TPU v7x, 256 devices: a whole 4x4x8 slice. The times are simulated.
256 devices in a mesh: col: 8 (over z_lo, core), dp: 32 (over z_hi, y, x).
Axes of the slice: x: 4, y: 4, z: 8 (z_hi: 2, z_lo: 4; z = z_hi * 4 + z_lo), core: 2. Of those that a mesh axis runs over, the one named last changes fastest.
Arguments:
- acts: bfloat16 [12288, 5120], P('dp', 'col'), may hold values from -6 to 6
- out_grad: bfloat16 [12288, 8192], P('dp', 'col'), may hold values from -6 to 6
- projection: bfloat16 [5120, 256], replicated, may hold values from -0.078125 to 0.078125
- weight: bfloat16 [5120, 8192], P('dp', 'col'), may hold values from -0.078125 to 0.078125
- m_codes: int32 [256, 8192], P('dp', 'col'), may hold values from -127 to 127
- m_exps: int32 [256, 256], P('dp', 'col'), may hold values from -16 to -9
- v_codes: int32 [256, 8192], P('dp', 'col'), may hold values from 1 to 127
- v_exps: int32 [256, 256], P('dp', 'col'), may hold values from -24 to -18
- next_acts: bfloat16 [12288, 5120], P('dp', 'col'), may hold values from -6 to 6
Outputs:
- next_out: bfloat16 [12288, 8192], P('dp', 'col')
- new_weight: bfloat16 [5120, 8192], P('dp', 'col')
- update: float32 [256, 8192], P('dp', 'col')
Inputs may be any that keep to these rules, and one draw needn't show every extreme that they name: `v_codes`: second moment mantissas are positive.
All inputs are finite; a program needn't handle non-finite values.
Results may differ from a plain program's by a relative error of at most 0.0051.
Values may be sent and summed in bfloat16 or wider, within the bound.
No kernel may reach another device: no remote copies, remote signals or barrier semaphores. Data moves between devices by JAX's collectives and lax.ppermute only.
A program may use at most 128 MiB of HBM per device.

v0:
```python
import jax
import jax.numpy as jnp
from jax import lax
from jax.sharding import Mesh
from jax.sharding import PartitionSpec as P

DP = ("dp_0", "dp_1", "dp_2")


learn_rate = 0.02
beta_one = 0.9
beta_two = 0.999
epsilon = 1e-08
correct_first = 0.9999734386011124
correct_second = 0.0952078528862904


def sent_to_all(shard, axis):
    size = lax.axis_size(axis)
    return lax.all_to_all(
        jnp.broadcast_to(shard[None], (size, *shard.shape)), axis, 0, 0, tiled=True
    )


def over_copies(shard, axis):
    everything = sent_to_all(shard, axis)
    return jnp.sum(everything, axis=0)


def cut_along(shard, dim, size):
    shape = shard.shape
    pieces = shard.reshape(*shape[:dim], size, shape[dim] // size, *shape[dim + 1 :])
    return jnp.moveaxis(pieces, dim, 0)


def sum_at_owner(shard, axis, dim):
    pieces = cut_along(shard, dim, lax.axis_size(axis))
    arrived = lax.all_to_all(pieces, axis, split_axis=0, concat_axis=0, tiled=True)
    return arrived.sum(axis=0)


def joined_along(pieces, dim):
    shape = list(pieces.shape[1:])
    shape[dim] *= pieces.shape[0]
    return jnp.moveaxis(pieces, 0, dim).reshape(shape)


def gather_in_order(shard, axes, sequence):
    pieces = shard[None]
    for k in sequence:
        pieces = lax.all_gather(pieces, axes[k], axis=0, tiled=True)
    block = [lax.axis_size(axes[k]) for k in reversed(sequence)]
    pieces = pieces.reshape(*block, *shard.shape)
    turned = sorted(range(len(sequence)), key=lambda place: sequence[len(sequence) - 1 - place])
    return pieces.transpose(*turned, *range(len(sequence), pieces.ndim)).reshape(-1, *shard.shape)


def gathered_by_axis(shard, axes, sequence, dim):
    return joined_along(gather_in_order(shard, axes, sequence), dim)


def collect(shard, axis, dim):
    pieces = sent_to_all(shard, axis)
    return joined_along(pieces, dim)


def decode(codes, exps):
    scale = jnp.exp2(exps.astype(jnp.float32))
    rows = codes.shape[0]
    values = (codes.astype(jnp.float32) / 128.0).reshape(
        rows, exps.shape[1], codes.shape[1] // exps.shape[1]
    )
    return (values * scale[:, :, None]).reshape(rows, codes.shape[1])


def body(acts, out_grad, projection, weight, m_codes, m_exps, v_codes, v_exps, next_acts):
    col_width = acts.shape[1]
    col_start = lax.axis_index("col") * col_width
    proj_cols = lax.dynamic_slice_in_dim(projection, col_start, col_width, 0)
    partial_value = jnp.dot(acts, proj_cols, preferred_element_type=jnp.float32)
    lowrank = over_copies(partial_value, "col").astype(jnp.bfloat16)
    tokens_all = acts.shape[0] * lax.axis_size(DP)
    grad = (
        sum_at_owner(
            lax.dot_general(
                lowrank, out_grad, (((0,), (0,)), ((), ())), preferred_element_type=jnp.float32
            ),
            DP,
            0,
        )
        / tokens_all
    )
    m_old = decode(m_codes, m_exps)
    v_old = decode(v_codes, v_exps)
    first = beta_one * m_old + (1.0 - beta_one) * grad
    second = beta_two * v_old + (1.0 - beta_two) * grad * grad
    update = first / correct_first / (jnp.sqrt(second / correct_second) + epsilon)
    direction = update.astype(jnp.bfloat16)
    full_next = lax.all_gather(next_acts, "col", axis=1, tiled=True)
    row_count = weight.shape[0]
    row_start = lax.axis_index(DP) * row_count
    old_full = gathered_by_axis(weight, DP, (0, 1, 2), 0)
    dir_full = collect(direction, DP, 0)
    delta_full = jnp.dot(projection, dir_full, preferred_element_type=jnp.float32)
    full_weight = (old_full.astype(jnp.float32) - learn_rate * delta_full).astype(jnp.bfloat16)
    new_weight = lax.dynamic_slice_in_dim(full_weight, row_start, row_count, 0)
    result = jnp.dot(full_next, full_weight, preferred_element_type=jnp.float32)
    return (result.astype(jnp.bfloat16), new_weight, update)


def solution(mesh):
    torus = Mesh(mesh.devices.reshape(mesh.shape["col"], 2, 4, 4), ("col", "dp_0", "dp_1", "dp_2"))
    return jax.shard_map(
        body,
        mesh=torus,
        in_specs=(
            P(DP, "col"),
            P(DP, "col"),
            P(),
            P(DP, "col"),
            P(DP, "col"),
            P(DP, "col"),
            P(DP, "col"),
            P(DP, "col"),
            P(DP, "col"),
        ),
        out_specs=(P(DP, "col"), P(DP, "col"), P(DP, "col")),
        check_vma=False,
    )
```

profile of v0, /device:TPU:2, one launch (start us, length us, event | category | flops | bytes accessed | tf_op | source)
XLA Modules:
  0.0 285.9 jit_solution(1275187251293601851)
XLA Ops:
  7.2 0.0 all-gather.5.cloned.1.call-start
  7.2 21.9 %all-gather = bf16[320,1024]{1,0:T(8,128)(2,1)} all-gather(bf16[160,1024]{1,0:T(8,128)(2,1)} %param.12), channel_id=2, replica_groups=mesh['col'=8,'dp_0'=2,'dp_1'=4,'dp_2'=4] {'dp_0'}, dimensions={0}, use_global_device_ids=true | all-gather | bytes 983040 | tf_op jit(solution)/shard_map/all_gather | solution.py:51
  29.2 0.0 all-gather.7.cloned.1.call-start
  29.2 39.9 %all-gather.5.cloned.1.call-done = bf16[8,160,1024]{2,1,0:T(8,128)(2,1)} async-done(((bf16[2,160,1024]{2,1,0:T(8,128)(2,1)}), bf16[8,160,1024]{2,1,0:T(8,128)(2,1)}) %all-gather.5.cloned.1.call-update) | async-done | bytes 2621456 | tf_op jit(solution)/shard_map/all_gather | solution.py:51
  69.2 1.4 convolution_bitcast_fusion.1
  70.6 0.2 copy.26
  70.8 2.0 broadcast_in_dim.7
  72.8 4.9 %all-to-all-start = ((f32[8,384,256]{2,1,0:T(8,128)}), f32[8,384,256]{2,1,0:T(8,128)}, u32[]{:S(2)}, u32[]{:S(2)}) async-start(f32[8,384,256]{2,1,0:T(8,128)} %broadcast_in_dim.7), calls=%async_computation | async-start | bytes 6291456 | tf_op jit(solution)/shard_map/all_to_all | solution.py:20
  77.7 0.0 all-gather.9.cloned.1.call-start
  77.8 0.7 all-gather.9.cloned.1.call-update
  78.5 70.9 %all-to-all-done = f32[8,384,256]{2,1,0:T(8,128)} async-done(((f32[8,384,256]{2,1,0:T(8,128)}), f32[8,384,256]{2,1,0:T(8,128)}, u32[]{:S(2)}, u32[]{:S(2)}) %all-to-all-start) | async-done | bytes 3145760 | tf_op jit(solution)/shard_map/all_to_all | solution.py:20
  149.4 2.9 reduce_sum.18
  152.2 2.4 convolution_bitcast_fusion
  154.6 11.0 %all-to-all-start.1 = ((f32[32,8,1024]{2,1,0:T(8,128)}), f32[32,8,1024]{2,1,0:T(8,128)}, u32[]{:S(2)}, u32[]{:S(2)}) async-start(f32[32,8,1024]{2,1,0:T(8,128)} %convolution_bitcast_fusion), calls=%async_computation.1 | async-start | bytes 2097152 | tf_op jit(solution)/shard_map/all_to_all | solution.py:38
  165.6 0.1 mul.78
  165.7 0.1 mul.79
  165.8 0.1 mul.70
  165.9 0.1 mul.71
  166.1 27.5 %all-to-all-done.1 = f32[32,8,1024]{2,1,0:T(8,128)} async-done(((f32[32,8,1024]{2,1,0:T(8,128)}), f32[32,8,1024]{2,1,0:T(8,128)}, u32[]{:S(2)}, u32[]{:S(2)}) %all-to-all-start.1) | async-done | bytes 1048608 | tf_op jit(solution)/shard_map/all_to_all | solution.py:38
  193.5 1.3 reduce_sum.19
  194.9 0.7 fusion.6
  195.5 0.9 broadcast_in_dim.8
  196.4 7.9 %all-to-all-start.2 = ((bf16[32,8,1024]{2,1,0:T(8,128)(2,1)}), bf16[32,8,1024]{2,1,0:T(8,128)(2,1)S(1)}, u32[]{:S(2)}, u32[]{:S(2)}) async-start(bf16[32,8,1024]{2,1,0:T(8,128)(2,1)} %broadcast_in_dim.8), calls=%async_computation.2 | async-start | bytes 1048576 | tf_op jit(solution)/shard_map/all_to_all | solution.py:20
  204.3 0.0 all-gather.7.cloned.1.call-done
  204.3 13.8 %convert_bitcast_fusion = f32[2,4,4,160,1024]{4,3,0,1,2:T(8,128)} fusion(bf16[4,4,2,160,1024]{4,3,2,1,0:T(8,128)(2,1)} %bitcast.26), kind=kLoop, calls=%fused_computation | loop fusion | flops 5242880 | bytes 31457280 | tf_op jit(solution)/shard_map/convert_element_type | solution.py:105
  218.1 16.5 %copy.25 = f32[2,4,4,160,1024]{4,3,2,1,0:T(8,128)} copy(f32[2,4,4,160,1024]{4,3,0,1,2:T(8,128)} %convert_bitcast_fusion) | data formatting | bytes 41943040 | tf_op jit(solution)/shard_map/convert_element_type | solution.py:105
  234.6 20.0 %copy.27 = f32[5120,1024]{0,1:T(8,128)} copy(f32[5120,1024]{1,0:T(8,128)} %bitcast.25) | data formatting | bytes 41943040 | tf_op jit(solution)/shard_map/convert_element_type | solution.py:105
  254.6 11.8 %fusion = bf16[5120,1024]{0,1:T(8,128)(2,1)} fusion(f32[5120,1024]{0,1:T(8,128)} %copy.27, bf16[5120,256]{1,0:T(8,128)(2,1)S(1)} %copy-done, bf16[32,8,1024]{2,1,0:T(8,128)(2,1)S(1)} %all-to-all-done.2), kind=kOutput, calls=%fused_computation.2 | convolution fusion | flops 2700083200 | bytes 34603008 | tf_op jit(solution)/shard_map/dot_general | solution.py:104
  266.4 9.5 %fusion.1 = bf16[384,1024]{0,1:T(8,128)(2,1)S(1)} fusion(bf16[5120,1024]{0,1:T(8,128)(2,1)} %fusion, bf16[384,5120]{1,0:T(8,128)(2,1)} %all-gather.9.cloned.1.call-done), kind=kOutput, calls=%fused_computation.5 | convolution fusion | flops 4026925056 | bytes 15204352 | tf_op jit(solution)/shard_map/dot_general | solution.py:107
  275.9 1.2 copy.28
  277.1 1.4 constant_dynamic-slice_fusion
  278.4 0.9 copy.29
  (18 shorter events, 0.1 us)
Async XLA Ops:
  7.2 62.0 %copy-start = (bf16[5120,256]{1,0:T(8,128)(2,1)S(1)}, bf16[5120,256]{1,0:T(8,128)(2,1)}, u32[]{:S(2)}) copy-start(bf16[5120,256]{1,0:T(8,128)(2,1)} %param.11) | copy-start | bytes 7864324
  7.2 61.9 %all-gather.5.cloned.1.call-start = ((), (), s32[]{:S(2)}) async-start(), calls=%async_computation.3 | async-start | bytes 3276800 | tf_op jit(solution)/shard_map/all_gather | solution.py:51
  29.2 175.1 %all-gather.7.cloned.1.call-start = ((), (), s32[]{:S(2)}) async-start(), calls=%async_computation.4 | async-start | bytes 13107200 | tf_op jit(solution)/shard_map/all_gather | solution.py:51
  69.1 96.5 %copy-start.4 = (s32[8,32]{1,0:T(8,128)S(1)}, s32[8,32]{1,0:T(8,128)}, u32[]{:S(2)}) copy-start(s32[8,32]{1,0:T(8,128)} %param.16) | copy-start | bytes 3076
  69.1 96.7 %copy-start.5 = (s32[8,32]{1,0:T(8,128)S(1)}, s32[8,32]{1,0:T(8,128)}, u32[]{:S(2)}) copy-start(s32[8,32]{1,0:T(8,128)} %param.14) | copy-start | bytes 3076
  69.2 125.7 %copy-start.2 = (s32[8,1024]{1,0:T(8,128)S(1)}, s32[8,1024]{1,0:T(8,128)}, u32[]{:S(2)}) copy-start(s32[8,1024]{1,0:T(8,128)} %param.15) | copy-start | bytes 98308
  69.2 125.7 %copy-start.3 = (s32[8,1024]{1,0:T(8,128)S(1)}, s32[8,1024]{1,0:T(8,128)}, u32[]{:S(2)}) copy-start(s32[8,1024]{1,0:T(8,128)} %param.13) | copy-start | bytes 98308
  72.8 79.4 %copy-start.1 = (bf16[384,1024]{1,0:T(8,128)(2,1)S(1)}, bf16[384,1024]{1,0:T(8,128)(2,1)}, u32[]{:S(2)}) copy-start(bf16[384,1024]{1,0:T(8,128)(2,1)} %param.10) | copy-start | bytes 2359300
  72.8 76.6 %all-to-all-start = ((f32[8,384,256]{2,1,0:T(8,128)}), f32[8,384,256]{2,1,0:T(8,128)}, u32[]{:S(2)}, u32[]{:S(2)}) async-start(f32[8,384,256]{2,1,0:T(8,128)} %broadcast_in_dim.7), calls=%async_computation | async-start | bytes 6291456 | tf_op jit(solution)/shard_map/all_to_all | solution.py:20
  77.7 188.7 %all-gather.9.cloned.1.call-start = ((), (), s32[]{:S(2)}) async-start(), calls=%async_computation.5 | async-start | bytes 4423680 | tf_op jit(solution)/shard_map/all_gather | solution.py:99
  154.6 39.0 %all-to-all-start.1 = ((f32[32,8,1024]{2,1,0:T(8,128)}), f32[32,8,1024]{2,1,0:T(8,128)}, u32[]{:S(2)}, u32[]{:S(2)}) async-start(f32[32,8,1024]{2,1,0:T(8,128)} %convolution_bitcast_fusion), calls=%async_computation.1 | async-start | bytes 2097152 | tf_op jit(solution)/shard_map/all_to_all | solution.py:38
  196.4 58.2 %all-to-all-start.2 = ((bf16[32,8,1024]{2,1,0:T(8,128)(2,1)}), bf16[32,8,1024]{2,1,0:T(8,128)(2,1)S(1)}, u32[]{:S(2)}, u32[]{:S(2)}) async-start(bf16[32,8,1024]{2,1,0:T(8,128)(2,1)} %broadcast_in_dim.8), calls=%async_computation.2 | async-start | bytes 1048576 | tf_op jit(solution)/shard_map/all_to_all | solution.py:20
Sparse Core Ops, SparseCore 0:
  29.3 39.7 all-gather.4
  70.9 111.1 all-gather.6
  184.0 67.3 all-gather.8
where the time goes:
time: 287 us; the launch traced here: 286 us
  waiting for transfers between devices  139 us (48%)
  local copies, waits for them, and re-layouts  43.4 us (15%)
  matrix products  25.1 us (9%)
  starting transfers between devices  23.9 us (8%)
  blocking collectives  21.9 us (8%)
  other arithmetic  18.6 us (6%)
  between operations  13.9 us (5%)
    all_to_all x2, waiting for transfers between devices, sent_to_all(): lax.all_to_all(jnp.broadcast_to(shard[None], (size, *shard.shape)), axis,...  70.9 us
    all_gather x2, waiting for transfers between devices, gather_in_order(): pieces = lax.all_gather(pieces, axes[k], axis=0, tiled=True)  39.9 us
    convert_element_type x2, local copies, waits for them, and re-layouts, body(): old_full.astype(jnp.float32) - learn_rate * delta_full  36.5 us
    all_to_all x1, waiting for transfers between devices, sum_at_owner(): lax.all_to_all(pieces, axis, split_axis=0, concat_axis=0, tiled=True)  27.5 us
    all_gather x1, blocking collectives, gather_in_order(): pieces = lax.all_gather(pieces, axes[k], axis=0, tiled=True)  21.9 us
    convert_element_type x1, other arithmetic, body(): old_full.astype(jnp.float32) - learn_rate * delta_full  13.8 us
    all_to_all x2, starting transfers between devices, sent_to_all(): lax.all_to_all(jnp.broadcast_to(shard[None], (size, *shard.shape)), axis,...  12.8 us
    dot_general x1, matrix products, body(): jnp.dot(projection, dir_full, preferred_element_type=jnp.float32)  11.8 us
  transfers between devices with their start and end apart: 6, of which 3 were waited for; matrix products, arithmetic and copies ran while one was open for 26% of the time, Pallas kernels for 0%

commit v1 on v0

v1 whole, which is shorter than its diff:
```python
import jax
import jax.numpy as jnp
from jax import lax
from jax.experimental import pallas as pl
from jax.experimental.pallas import tpu as pltpu
from jax.sharding import Mesh
from jax.sharding import PartitionSpec as P

learn_rate = 0.02
beta_one = 0.9
beta_two = 0.999
epsilon = 1e-08
correct_first = 0.9999734386011124
correct_second = 0.0952078528862904

bf16 = jnp.bfloat16
f32 = jnp.float32


PLANE = ("y", "x")
FIRST_TOKENS = 96


def shift(value, axis, step=1):
    size = lax.axis_size(axis)
    return lax.ppermute(value, axis, [(i, (i + step) % size) for i in range(size)])


def swap(value, axes):
    return lax.all_to_all(value, axes, 0, 0, tiled=True)


def gather(block, axes):
    size = lax.axis_size(axes)
    return swap(jnp.broadcast_to(block[None], (size, *block.shape)), axes)


def around(block, axis):
    left = shift(block, axis, 1)
    right = shift(block, axis, -1)
    far = shift(block, axis, 2)
    return [block, left, far, right]


def plane_shift(value, outer, step):
    pairs = []
    for k in range(2):
        for y in range(4):
            for x in range(4):
                to_y, to_x = ((y + step) % 4, x) if (k == 0) == outer else (y, (x + step) % 4)
                pairs.append(((k * 4 + y) * 4 + x, (k * 4 + to_y) * 4 + to_x))
    return lax.ppermute(value, ("k", "y", "x"), pairs)


def plane_around(block, outer):
    left = plane_shift(block, outer, 1)
    right = plane_shift(block, outer, -1)
    far = plane_shift(block, outer, 2)
    return [block, left, far, right]


def decode(codes, exps):
    scale = jnp.exp2(exps.astype(f32))
    rows = codes.shape[0]
    values = (codes.astype(f32) / 128.0).reshape(rows, exps.shape[1], codes.shape[1] // exps.shape[1])
    return (values * scale[:, :, None]).reshape(rows, codes.shape[1])


def pair_order(mine, other, me):
    return jnp.where(me == 0, jnp.concatenate([mine, other], 0), jnp.concatenate([other, mine], 0))


def mm(a, b):
    return jnp.dot(a, b, preferred_element_type=f32)


def side_kernel(last, place, *refs):
    pieces, xs, proj = refs[:4], (refs[4:12], refs[12:20]), refs[20]
    if last:
        acc_in, low_in, direction, out = refs[21:25]
    else:
        acc, low = refs[21:23]
    w, xb, pb, wsem, xsem, psem = refs[-6:]
    rows, _ = pieces[0].shape[1:]
    feat = xb.shape[1] // 4
    side_h, k, z, y, x = (place[i] for i in range(5))

    def w_copy(src, to_y, to_x):
        at = pl.ds(pl.multiple_of(to_y * feat + to_x * rows, 32), rows)
        return pltpu.make_async_copy(src, w.at[at], wsem.at[to_y, to_x])

    def x_copy(src, chunk, n):
        at = pl.ds(0, FIRST_TOKENS) if n == 0 else pl.ds(FIRST_TOKENS, src.shape[0])
        to = pl.ds(pl.multiple_of(chunk * feat, 128), feat)
        return pltpu.make_async_copy(src, xb.at[at, to], xsem.at[chunk, n])

    def p_copy(i):
        return pltpu.make_async_copy(proj.at[4 * side_h + i], pb.at[pl.ds(i * feat, feat)], psem.at[i])

    for s in range(4):
        from_z = lax.rem(z - s + 4, 4)

        @pl.when(from_z // 2 == side_h)
        def _():
            for n in range(2):
                x_copy(xs[n][s], 2 * lax.rem(from_z, 2) + k, n).start()
                x_copy(xs[n][4 + s], 2 * lax.rem(from_z, 2) + 1 - k, n).start()

    for i in range(4):
        p_copy(i).start()
    for s in range(4):
        for t in range(4):
            back_y = jnp.where(k == 0, s, t)
            back_x = jnp.where(k == 0, t, s)
            w_copy(pieces[s].at[t], lax.rem(y - back_y + 4, 4), lax.rem(x - back_x + 4, 4)).start()
    for i in range(2):
        for j in (2 * i, 2 * i + 1):
            for n in range(2):
                x_copy(xs[n][0], j, n).wait()
            p_copy(j).wait()
            for t in range(4):
                w_copy(pieces[0].at[0], j, t).wait()
        at = slice(2 * i * feat, 2 * (i + 1) * feat)
        feats = xb[:, at]
        a = mm(feats, w[at])
        b = mm(feats, pb[at])
        if i == 0:
            total, total_low = (acc_in[...] + a, low_in[...] + b) if last else (a, b)
        else:
            total, total_low = total + a, total_low + b
    if last:
        out[...] = (total - learn_rate * mm(total_low.astype(bf16), direction[...])).astype(bf16)
    else:
        acc[...] = total
        low[...] = total_low


def side(place, pieces, xs, proj, *rest):
    _, _, width = pieces[0].shape
    feat = xs[0].shape[1]
    tok = xs[0].shape[0] + xs[8].shape[0]
    rank = proj.shape[-1]
    last = len(rest) > 0
    vmem = pl.BlockSpec(memory_space=pltpu.VMEM)
    hbm = pl.BlockSpec(memory_space=pl.ANY)
    if last:
        outs = jax.ShapeDtypeStruct((tok, width), bf16)
        out_specs = vmem
    else:
        outs = [jax.ShapeDtypeStruct((tok, width), f32), jax.ShapeDtypeStruct((tok, rank), f32)]
        out_specs = [vmem, vmem]
    return pl.pallas_call(
        lambda *refs: side_kernel(last, *refs),
        in_specs=[pl.BlockSpec(memory_space=pltpu.SMEM), *[hbm] * 21, *[vmem] * len(rest)],
        out_specs=out_specs,
        out_shape=outs,
        scratch_shapes=[
            pltpu.VMEM((4 * feat, width), bf16),
            pltpu.VMEM((tok, 4 * feat), bf16),
            pltpu.VMEM((4 * feat, rank), bf16),
            pltpu.SemaphoreType.DMA((4, 4)),
            pltpu.SemaphoreType.DMA((4, 2)),
            pltpu.SemaphoreType.DMA((4,)),
        ],
        compiler_params=pltpu.CompilerParams(vmem_limit_bytes=32 << 20),
        name="last_product" if last else "first_product",
    )(place, *pieces, *xs, proj, *rest)


def body(acts, out_grad, projection, weight, m_codes, m_exps, v_codes, v_exps, next_acts):
    k = lax.axis_index("k")
    z = lax.axis_index("z")
    h = lax.axis_index("h")
    tok, feat = acts.shape
    half = tok // 2
    rank = projection.shape[1]
    rows, width = weight.shape
    tokens_all = tok * lax.axis_size(("h", "y", "x"))

    mine = lax.dynamic_slice_in_dim(acts, k * half, half, 0)
    theirs = lax.dynamic_slice_in_dim(acts, (1 - k) * half, half, 0)
    got = shift(theirs, "k")
    p_mine = lax.dynamic_slice_in_dim(projection, (2 * z + k) * feat, feat, 0)
    p_got = lax.dynamic_slice_in_dim(projection, (2 * z + 1 - k) * feat, feat, 0)
    part = mm(mine, p_mine) + mm(got, p_got)
    low = swap(part.reshape(4, half // 4, rank), "z").sum(axis=0).astype(bf16)
    low = gather(low, "z").reshape(half, rank)
    lowrank = pair_order(low, shift(low, "k"), k)

    grad_part = lax.dot_general(lowrank, out_grad, (((0,), (0,)), ((), ())), preferred_element_type=f32)
    q = lax.axis_size(PLANE)
    own = rank // q // 2
    cut = grad_part.astype(bf16).reshape(2, q, own, width).transpose(1, 0, 2, 3).reshape(q, 2 * own, width)
    plane = swap(cut, PLANE).astype(f32).sum(axis=0)
    grad = (plane + shift(plane, "h")) / tokens_all

    moments = jnp.concatenate([decode(m_codes, m_exps), decode(v_codes, v_exps)], 0)
    other = shift(jnp.concatenate([weight, moments.astype(bf16)], 0), "h")
    shard = (weight, other[:rows])
    other = other[rows:].astype(f32)
    m_old = pair_order(moments[:own], other[:own], h)
    v_old = pair_order(moments[own:], other[own:], h)
    first = beta_one * m_old + (1.0 - beta_one) * grad
    second = beta_two * v_old + (1.0 - beta_two) * grad * grad
    both = first / correct_first / (jnp.sqrt(second / correct_second) + epsilon)
    update = jnp.where(h == 0, both[:own], both[own:])
    direction = gather(both.astype(bf16), PLANE)
    direction = direction.reshape(q, 2, own, width).transpose(1, 0, 2, 3).reshape(rank, width)

    xs = []
    for part in (next_acts[:FIRST_TOKENS], next_acts[FIRST_TOKENS:]):
        ring = around(part, "z")
        xs += ring
        xs += [shift(piece, "k") for piece in ring]

    proj = projection.reshape(8, feat, rank)
    rest = ()
    for s in (0, 1):
        block = jnp.stack(plane_around(shard[s], False))
        full = plane_around(block, True)
        place = jnp.stack([jnp.where(h == s, 0, 1), k, z, lax.axis_index("y"), lax.axis_index("x")]).astype(jnp.int32)
        rest = side(place, full, xs, proj, *rest)
        if s == 0:
            rest = (*rest, direction)
    out = rest

    p_rows = lax.dynamic_slice_in_dim(projection, lax.axis_index(("h", "y", "x")) * rows, rows, 0)
    new_weight = (weight.astype(f32) - learn_rate * mm(p_rows, direction)).astype(bf16)
    return (out, new_weight, update)


def solution(mesh):
    torus = Mesh(mesh.devices.reshape(mesh.shape["col"] // 2, 2, 2, 4, 4), ("z", "k", "h", "y", "x"))
    both = P(("h", "y", "x"), ("z", "k"))
    return jax.shard_map(
        body,
        mesh=torus,
        in_specs=(both, both, P(), both, both, both, both, both, both),
        out_specs=(both, both, both),
        check_vma=False,
    )
```

time: 287 us -> 192 us (0.67)
  the two profiles are of different devices: /device:TPU:2 before, /device:TPU:195 now
where the time goes in v1:
time: 192 us; the launch traced here: 191 us
  starting transfers between devices  70.1 us (37%)
  waiting for transfers between devices  49.9 us (26%)
  local copies, waits for them, and re-layouts  37.7 us (20%)
  Pallas kernels  15.6 us (8%)
  other arithmetic  10.7 us (6%)
  matrix products  5.67 us (3%)
    unnamed x104, local copies, waits for them, and re-layouts  29.6 us
    all_to_all x4, starting transfers between devices, swap(): return lax.all_to_all(value, axes, 0, 0, tiled=True)  27.3 us
    all_to_all x4, waiting for transfers between devices, swap(): return lax.all_to_all(value, axes, 0, 0, tiled=True)  25.5 us
    ppermute x18, starting transfers between devices, shift(): lax.ppermute(value, axis, [(i, (i + step) % size) for i in range(size)])  25.2 us
    ppermute x12, waiting for transfers between devices, plane_shift(): return lax.ppermute(value, ('k', 'y', 'x'), pairs)  20.6 us
    ppermute x12, starting transfers between devices, plane_shift(): return lax.ppermute(value, ('k', 'y', 'x'), pairs)  17.6 us
    pallas_call x2, Pallas kernels, side(): pl.pallas_call(lambda *refs: side_kernel(last, *refs), in_specs=[pl.Block...  15.6 us
    dot_general x3, matrix products, mm(): return jnp.dot(a, b, preferred_element_type=f32)  5.2 us
  transfers between devices with their start and end apart: 34, of which 6 were waited for; matrix products, arithmetic and copies ran while one was open for 12% of the time, Pallas kernels for 4%

profile of v1, /device:TPU:195, one launch (start us, length us, event | category | flops | bytes accessed | tf_op | source)
XLA Modules:
  0.0 190.7 jit_solution(13889405718525553411)
XLA Ops:
  2.5 1.2 collective-permute-start.8
  3.7 1.3 collective-permute-start.21
  5.0 2.6 %collective-permute-start.22 = (bf16[160,1024]{1,0:T(8,128)(2,1)}, bf16[160,1024]{1,0:T(8,128)(2,1)}, u32[]{:S(2)}, u32[]{:S(2)}) collective-permute-start(bf16[160,1024]{1,0:T(8,128)(2,1)} %param.12), channel_id=1, source_target_pairs={{0,2},{1,3},{2,0},{3,1},{4,6},{5,7},{6,4},{7,5},{8,10},{9,11},{10,... | collective-permute-start | bytes 983048 | tf_op jit(solution)/shard_map/ppermute | solution.py:52
  10.1 1.3 fusion.3
  12.5 2.6 %collective-permute-start.23 = (bf16[160,1024]{1,0:T(8,128)(2,1)S(1)}, bf16[160,1024]{1,0:T(8,128)(2,1)}, u32[]{:S(2)}, u32[]{:S(2)}) collective-permute-start(bf16[160,1024]{1,0:T(8,128)(2,1)S(1)} %copy-done.45), channel_id=1, source_target_pairs={{0,3},{1,0},{2,1},{3,2},{4,7},{5,4},{6,5},{7,6},{8,11},{9,8},{10,9... | collective-permute-start | bytes 983048 | tf_op jit(solution)/shard_map/ppermute | solution.py:52
  15.1 1.9 convolution_add_fusion
  17.0 4.5 %all-to-all-start = ((f32[4,48,256]{2,1,0:T(8,128)}), f32[4,48,256]{2,1,0:T(8,128)S(1)}, u32[]{:S(2)}, u32[]{:S(2)}) async-start(f32[4,48,256]{2,1,0:T(8,128)} %bitcast.15), calls=%async_computation | async-start | bytes 393216 | tf_op jit(solution)/shard_map/all_to_all | solution.py:30
  22.3 1.2 collective-permute-start
  23.8 14.5 %all-to-all-done = f32[4,48,256]{2,1,0:T(8,128)S(1)} async-done(((f32[4,48,256]{2,1,0:T(8,128)}), f32[4,48,256]{2,1,0:T(8,128)S(1)}, u32[]{:S(2)}, u32[]{:S(2)}) %all-to-all-start) | async-done | bytes 196640 | tf_op jit(solution)/shard_map/all_to_all | solution.py:30
  39.0 9.8 %all-to-all-start.1 = ((bf16[4,48,256]{2,1,0:T(8,128)(2,1)}), bf16[4,48,256]{2,1,0:T(8,128)(2,1)S(1)}, u32[]{:S(2)}, u32[]{:S(2)}) async-start(bf16[4,48,256]{2,1,0:T(8,128)(2,1)} %broadcast_in_dim.4), calls=%async_computation.1 | async-start | bytes 196608 | tf_op jit(solution)/shard_map/all_to_all | solution.py:30
  48.8 1.3 collective-permute-start.14
  50.9 2.3 %pad_maximum_fusion.1.refs_1_ = bf16[4,160,1024]{2,1,0:T(8,128)(2,1)} fusion(bf16[1,160,1024]{2,1,0:T(8,128)(2,1)} %bitcast.14, bf16[1,160,1024]{2,1,0:T(8,128)(2,1)} %bitcast.13, bf16[1,160,1024]{2,1,0:T(8,128)(2,1)S(1)} %bitcast.37, bf16[1,160,1024]{2,1,0:T(8,128)(2,1)S(1)} %bitcast.35), kind=kLoop, calls=%fused_computation.1 | loop fusion | flops 1966080 | bytes 2621440 | tf_op jit(solution)/shard_map/stack | solution.py:219
  55.8 1.9 slice_bitcast_fusion
  59.4 17.2 %collective-permute-start.17 = (bf16[288,640]{1,0:T(8,128)(2,1)S(1)}, bf16[288,640]{1,0:T(8,128)(2,1)S(1)}, u32[]{:S(2)}, u32[]{:S(2)}) collective-permute-start(bf16[288,640]{1,0:T(8,128)(2,1)S(1)} %slice.26.refs_13_), channel_id=1, source_target_pairs={{0,32},{32,0},{1,33},{33,1},{2,34},{34,2},{3,35},{35,3},{4,36},{36... | collective-permute-start | bytes 1105928 | tf_op jit(solution)/shard_map/ppermute | solution.py:26
  77.9 6.4 %all-to-all-start.2 = ((bf16[16,16,1024]{2,1,0:T(8,128)(2,1)}), bf16[16,16,1024]{2,1,0:T(8,128)(2,1)S(1)}, u32[]{:S(2)}, u32[]{:S(2)}) async-start(bf16[16,16,1024]{2,1,0:T(8,128)(2,1)} %bitcast.30), calls=%async_computation.2 | async-start | bytes 1048576 | tf_op jit(solution)/shard_map/all_to_all | solution.py:30
  84.3 2.8 %collective-permute-start.2 = (bf16[160,1024]{1,0:T(8,128)(2,1)}, bf16[160,1024]{1,0:T(8,128)(2,1)}, u32[]{:S(2)}, u32[]{:S(2)}) collective-permute-start(bf16[160,1024]{1,0:T(8,128)(2,1)} %get-tuple-element.14), channel_id=1, source_target_pairs={{0,2},{1,3},{2,0},{3,1},{4,6},{5,7},{6,4},{7,5},{8,10},{9,11},{10,... | collective-permute-start | bytes 983048 | tf_op jit(solution)/shard_map/ppermute | solution.py:52
  88.4 2.4 %collective-permute-start.3 = (bf16[160,1024]{1,0:T(8,128)(2,1)}, bf16[160,1024]{1,0:T(8,128)(2,1)S(1)}, u32[]{:S(2)}, u32[]{:S(2)}) collective-permute-start(bf16[160,1024]{1,0:T(8,128)(2,1)} %get-tuple-element.14), channel_id=1, source_target_pairs={{0,3},{1,0},{2,1},{3,2},{4,7},{5,4},{6,5},{7,6},{8,11},{9,8},{10,9... | collective-permute-start | bytes 983048 | tf_op jit(solution)/shard_map/ppermute | solution.py:52
  90.8 6.6 %collective-permute-done.2 = bf16[160,1024]{1,0:T(8,128)(2,1)} collective-permute-done((bf16[160,1024]{1,0:T(8,128)(2,1)}, bf16[160,1024]{1,0:T(8,128)(2,1)}, u32[]{:S(2)}, u32[]{:S(2)}) %collective-permute-start.2) | collective-permute-done | bytes 327712 | tf_op jit(solution)/shard_map/ppermute | solution.py:52
  97.5 2.4 %collective-permute-done.3 = bf16[160,1024]{1,0:T(8,128)(2,1)S(1)} collective-permute-done((bf16[160,1024]{1,0:T(8,128)(2,1)}, bf16[160,1024]{1,0:T(8,128)(2,1)S(1)}, u32[]{:S(2)}, u32[]{:S(2)}) %collective-permute-start.3) | collective-permute-done | bytes 327712 | tf_op jit(solution)/shard_map/ppermute | solution.py:52
  99.8 1.6 collective-permute-start.25
  103.9 2.7 %pad_maximum_fusion.refs_1_ = bf16[4,160,1024]{2,1,0:T(8,128)(2,1)} fusion(bf16[1,160,1024]{2,1,0:T(8,128)(2,1)} %bitcast.38, bf16[1,160,1024]{2,1,0:T(8,128)(2,1)} %bitcast.7, bf16[1,160,1024]{2,1,0:T(8,128)(2,1)} %bitcast.6, bf16[1,160,1024]{2,1,0:T(8,128)(2,1)} %get-tuple-element.13), kind=kLoop, calls=%fused_computation | loop fusion | flops 1966080 | bytes 2621440 | tf_op jit(solution)/shard_map/stack | solution.py:219
  107.1 3.8 %collective-permute-done.29 = f32[16,1024]{1,0:T(8,128)S(1)} collective-permute-done((f32[16,1024]{1,0:T(8,128)S(1)}, f32[16,1024]{1,0:T(8,128)S(1)}, u32[]{:S(2)}, u32[]{:S(2)}) %collective-permute-start.29) | collective-permute-done | bytes 65568 | tf_op jit(solution)/shard_map/ppermute | solution.py:26
  111.3 1.9 collective-permute-start.6
  115.5 6.6 %all-to-all-start.3 = ((bf16[16,16,1024]{2,1,0:T(8,128)(2,1)}), bf16[16,16,1024]{2,1,0:T(8,128)(2,1)}, u32[]{:S(2)}, u32[]{:S(2)}) async-start(bf16[16,16,1024]{2,1,0:T(8,128)(2,1)} %broadcast_in_dim.5), calls=%async_computation.3 | async-start | bytes 1048576 | tf_op jit(solution)/shard_map/all_to_all | solution.py:30
  122.3 1.4 slice_select_fusion
  123.7 11.6 %collective-permute-done.26.refs_4_ = bf16[4,160,1024]{2,1,0:T(8,128)(2,1)} collective-permute-done((bf16[4,160,1024]{2,1,0:T(8,128)(2,1)}, bf16[4,160,1024]{2,1,0:T(8,128)(2,1)}, u32[]{:S(2)}, u32[]{:S(2)}) %collective-permute-start.26) | collective-permute-done | bytes 1310752 | tf_op jit(solution)/shard_map/ppermute | solution.py:52
  147.5 7.1 %first_product.1 = (f32[384,1024]{1,0:T(8,128)S(1)}, f32[384,256]{1,0:T(8,128)S(1)}) custom-call(s32[5]{0:T(128)S(1)} %stack.70.refs_0_, bf16[4,160,1024]{2,1,0:T(8,128)(2,1)} %pad_maximum_fusion.1.refs_1_, bf16[4,160,1024]{2,1,0:T(8,128)(2,1)} %collective-permute-done.24.refs_2_, bf16[4,160,1024]{2,1,0:T(8,128)(2,1)} %collective-permute-done.25.refs_3_, ...), custom_call_target="tpu_custom_call" | custom-call | tf_op jit(solution)/shard_map/first_product/pallas_call | solution.py:152
  154.7 1.1 copy-done.5
  156.6 11.0 %all-to-all-done.3 = bf16[16,16,1024]{2,1,0:T(8,128)(2,1)} async-done(((bf16[16,16,1024]{2,1,0:T(8,128)(2,1)}), bf16[16,16,1024]{2,1,0:T(8,128)(2,1)}, u32[]{:S(2)}, u32[]{:S(2)}) %all-to-all-start.3) | async-done | bytes 524320 | tf_op jit(solution)/shard_map/all_to_all | solution.py:30
  167.6 1.2 copy.13
  168.8 2.0 %fusion.1 = bf16[160,1024]{1,0:T(8,128)(2,1)} fusion(bf16[256,1024]{1,0:T(8,128)(2,1)S(1)} %bitcast.33, bf16[160,1024]{1,0:T(8,128)(2,1)} %param.12, bf16[5120,256]{1,0:T(8,128)(2,1)S(1)} %copy-done.1, s32[]{:T(128)S(6)} %select_n.61), kind=kOutput, calls=%fused_computation.5 | convolution fusion | flops 84541440 | bytes 1261572 | tf_op jit(solution)/shard_map/dot_general | solution.py:74
  182.1 8.5 %last_product.1 = bf16[384,1024]{1,0:T(8,128)(2,1)} custom-call(s32[5]{0:T(128)S(1)} %stack.63.refs_0_, bf16[4,160,1024]{2,1,0:T(8,128)(2,1)} %pad_maximum_fusion.refs_1_, bf16[4,160,1024]{2,1,0:T(8,128)(2,1)} %collective-permute-done.4.refs_2_, bf16[4,160,1024]{2,1,0:T(8,128)(2,1)} %collective-permute-done.5.refs_3_, ...), custom_call_target="tpu_custom_call" | custom-call | tf_op jit(solution)/shard_map/last_product/pallas_call | solution.py:152
  (172 shorter events, 45.1 us)
Async XLA Ops:
  1.7 20.6 %collective-permute-start.7 = (bf16[96,640]{1,0:T(8,128)(2,1)S(1)}, bf16[96,640]{1,0:T(8,128)(2,1)S(1)}, u32[]{:S(2)}, u32[]{:S(2)}) collective-permute-start(bf16[96,640]{1,0:T(8,128)(2,1)S(1)} %slice.25.refs_5_), channel_id=1, source_target_pairs={{0,64},{64,128},{128,192},{192,0},{1,65},{65,129},{129,193},{193,1... | collective-permute-start | bytes 368648 | tf_op jit(solution)/shard_map/ppermute | solution.py:26
  2.5 21.0 %collective-permute-start.8 = (bf16[96,640]{1,0:T(8,128)(2,1)S(1)}, bf16[96,640]{1,0:T(8,128)(2,1)S(1)}, u32[]{:S(2)}, u32[]{:S(2)}) collective-permute-start(bf16[96,640]{1,0:T(8,128)(2,1)S(1)} %slice.25.refs_5_), channel_id=1, source_target_pairs={{0,128},{64,192},{128,0},{192,64},{1,129},{65,193},{129,1},{193,65... | collective-permute-start | bytes 368648 | tf_op jit(solution)/shard_map/ppermute | solution.py:26
  3.7 45.2 %collective-permute-start.21 = (bf16[160,1024]{1,0:T(8,128)(2,1)}, bf16[160,1024]{1,0:T(8,128)(2,1)S(1)}, u32[]{:S(2)}, u32[]{:S(2)}) collective-permute-start(bf16[160,1024]{1,0:T(8,128)(2,1)} %param.12), channel_id=1, source_target_pairs={{0,1},{1,2},{2,3},{3,0},{4,5},{5,6},{6,7},{7,4},{8,9},{9,10},{10,1... | collective-permute-start | bytes 983048 | tf_op jit(solution)/shard_map/ppermute | solution.py:52
  5.0 45.1 %collective-permute-start.22 = (bf16[160,1024]{1,0:T(8,128)(2,1)}, bf16[160,1024]{1,0:T(8,128)(2,1)}, u32[]{:S(2)}, u32[]{:S(2)}) collective-permute-start(bf16[160,1024]{1,0:T(8,128)(2,1)} %param.12), channel_id=1, source_target_pairs={{0,2},{1,3},{2,0},{3,1},{4,6},{5,7},{6,4},{7,5},{8,10},{9,11},{10,... | collective-permute-start | bytes 983048 | tf_op jit(solution)/shard_map/ppermute | solution.py:52
  12.5 38.3 %collective-permute-start.23 = (bf16[160,1024]{1,0:T(8,128)(2,1)S(1)}, bf16[160,1024]{1,0:T(8,128)(2,1)}, u32[]{:S(2)}, u32[]{:S(2)}) collective-permute-start(bf16[160,1024]{1,0:T(8,128)(2,1)S(1)} %copy-done.45), channel_id=1, source_target_pairs={{0,3},{1,0},{2,1},{3,2},{4,7},{5,4},{6,5},{7,6},{8,11},{9,8},{10,9... | collective-permute-start | bytes 983048 | tf_op jit(solution)/shard_map/ppermute | solution.py:52
  17.0 21.3 %all-to-all-start = ((f32[4,48,256]{2,1,0:T(8,128)}), f32[4,48,256]{2,1,0:T(8,128)S(1)}, u32[]{:S(2)}, u32[]{:S(2)}) async-start(f32[4,48,256]{2,1,0:T(8,128)} %bitcast.15), calls=%async_computation | async-start | bytes 393216 | tf_op jit(solution)/shard_map/all_to_all | solution.py:30
  22.3 33.2 %collective-permute-start = (bf16[176,1024]{1,0:T(8,128)(2,1)}, bf16[176,1024]{1,0:T(8,128)(2,1)}, u32[]{:S(2)}, u32[]{:S(2)}) collective-permute-start(bf16[176,1024]{1,0:T(8,128)(2,1)} %pad_maximum_fusion.2), channel_id=1, source_target_pairs={{0,16},{16,0},{1,17},{17,1},{2,18},{18,2},{3,19},{19,3},{4,20},{20... | collective-permute-start | bytes 1081352 | tf_op jit(solution)/shard_map/ppermute | solution.py:26
  23.5 25.3 %collective-permute-start.9 = (bf16[96,640]{1,0:T(8,128)(2,1)S(1)}, bf16[96,640]{1,0:T(8,128)(2,1)S(1)}, u32[]{:S(2)}, u32[]{:S(2)}) collective-permute-start(bf16[96,640]{1,0:T(8,128)(2,1)S(1)} %slice.25.refs_5_), channel_id=1, source_target_pairs={{0,192},{64,0},{128,64},{192,128},{1,193},{65,1},{129,65},{193,129... | collective-permute-start | bytes 368648 | tf_op jit(solution)/shard_map/ppermute | solution.py:26
  39.0 16.6 %all-to-all-start.1 = ((bf16[4,48,256]{2,1,0:T(8,128)(2,1)}), bf16[4,48,256]{2,1,0:T(8,128)(2,1)S(1)}, u32[]{:S(2)}, u32[]{:S(2)}) async-start(bf16[4,48,256]{2,1,0:T(8,128)(2,1)} %broadcast_in_dim.4), calls=%async_computation.1 | async-start | bytes 196608 | tf_op jit(solution)/shard_map/all_to_all | solution.py:30
  48.8 4.4 %collective-permute-start.10 = (bf16[96,640]{1,0:T(8,128)(2,1)S(1)}, bf16[96,640]{1,0:T(8,128)(2,1)S(1)}, u32[]{:S(2)}, u32[]{:S(2)}) collective-permute-start(bf16[96,640]{1,0:T(8,128)(2,1)S(1)} %slice.25.refs_5_), channel_id=1, source_target_pairs={{0,32},{32,0},{1,33},{33,1},{2,34},{34,2},{3,35},{35,3},{4,36},{36... | collective-permute-start | bytes 368648 | tf_op jit(solution)/shard_map/ppermute | solution.py:26
  48.8 10.6 %collective-permute-start.14 = (bf16[288,640]{1,0:T(8,128)(2,1)S(1)}, bf16[288,640]{1,0:T(8,128)(2,1)S(1)}, u32[]{:S(2)}, u32[]{:S(2)}) collective-permute-start(bf16[288,640]{1,0:T(8,128)(2,1)S(1)} %slice.26.refs_13_), channel_id=1, source_target_pairs={{0,64},{64,128},{128,192},{192,0},{1,65},{65,129},{129,193},{193,1... | collective-permute-start | bytes 1105928 | tf_op jit(solution)/shard_map/ppermute | solution.py:26
  50.1 4.2 %collective-permute-start.11 = (bf16[96,640]{1,0:T(8,128)(2,1)S(1)}, bf16[96,640]{1,0:T(8,128)(2,1)S(1)}, u32[]{:S(2)}, u32[]{:S(2)}) collective-permute-start(bf16[96,640]{1,0:T(8,128)(2,1)S(1)} %collective-permute-done.7.refs_6_), channel_id=1, source_target_pairs={{0,32},{32,0},{1,33},{33,1},{2,34},{34,2},{3,35},{35,3},{4,36},{36... | collective-permute-start | bytes 368648 | tf_op jit(solution)/shard_map/ppermute | solution.py:26
  50.8 4.4 %collective-permute-start.12 = (bf16[96,640]{1,0:T(8,128)(2,1)S(1)}, bf16[96,640]{1,0:T(8,128)(2,1)S(1)}, u32[]{:S(2)}, u32[]{:S(2)}) collective-permute-start(bf16[96,640]{1,0:T(8,128)(2,1)S(1)} %collective-permute-done.8.refs_7_), channel_id=1, source_target_pairs={{0,32},{32,0},{1,33},{33,1},{2,34},{34,2},{3,35},{35,3},{4,36},{36... | collective-permute-start | bytes 368648 | tf_op jit(solution)/shard_map/ppermute | solution.py:26
  53.8 57.5 %collective-permute-start.24 = (bf16[4,160,1024]{2,1,0:T(8,128)(2,1)}, bf16[4,160,1024]{2,1,0:T(8,128)(2,1)}, u32[]{:S(2)}, u32[]{:S(2)}) collective-permute-start(bf16[4,160,1024]{2,1,0:T(8,128)(2,1)} %pad_maximum_fusion.1.refs_1_), channel_id=1, source_target_pairs={{0,4},{1,5},{2,6},{3,7},{4,8},{5,9},{6,10},{7,11},{8,12},{9,13},{1... | collective-permute-start | bytes 3932168 | tf_op jit(solution)/shard_map/ppermute | solution.py:52
  54.9 29.4 %collective-permute-start.15 = (bf16[288,640]{1,0:T(8,128)(2,1)S(1)}, bf16[288,640]{1,0:T(8,128)(2,1)S(1)}, u32[]{:S(2)}, u32[]{:S(2)}) collective-permute-start(bf16[288,640]{1,0:T(8,128)(2,1)S(1)} %slice.26.refs_13_), channel_id=1, source_target_pairs={{0,128},{64,192},{128,0},{192,64},{1,129},{65,193},{129,1},{193,65... | collective-permute-start | bytes 1105928 | tf_op jit(solution)/shard_map/ppermute | solution.py:26
  55.5 21.0 %collective-permute-start.28 = (bf16[192,256]{1,0:T(8,128)(2,1)S(1)}, bf16[192,256]{1,0:T(8,128)(2,1)S(1)}, u32[]{:S(2)}, u32[]{:S(2)}) collective-permute-start(bf16[192,256]{1,0:T(8,128)(2,1)S(1)} %bitcast.39), channel_id=1, source_target_pairs={{0,32},{32,0},{1,33},{33,1},{2,34},{34,2},{3,35},{35,3},{4,36},{36... | collective-permute-start | bytes 294920 | tf_op jit(solution)/shard_map/ppermute | solution.py:26
  58.4 28.7 %collective-permute-start.16 = (bf16[288,640]{1,0:T(8,128)(2,1)S(1)}, bf16[288,640]{1,0:T(8,128)(2,1)}, u32[]{:S(2)}, u32[]{:S(2)}) collective-permute-start(bf16[288,640]{1,0:T(8,128)(2,1)S(1)} %slice.26.refs_13_), channel_id=1, source_target_pairs={{0,192},{64,0},{128,64},{192,128},{1,193},{65,1},{129,65},{193,129... | collective-permute-start | bytes 1105928 | tf_op jit(solution)/shard_map/ppermute | solution.py:26
  59.4 28.2 %collective-permute-start.17 = (bf16[288,640]{1,0:T(8,128)(2,1)S(1)}, bf16[288,640]{1,0:T(8,128)(2,1)S(1)}, u32[]{:S(2)}, u32[]{:S(2)}) collective-permute-start(bf16[288,640]{1,0:T(8,128)(2,1)S(1)} %slice.26.refs_13_), channel_id=1, source_target_pairs={{0,32},{32,0},{1,33},{33,1},{2,34},{34,2},{3,35},{35,3},{4,36},{36... | collective-permute-start | bytes 1105928 | tf_op jit(solution)/shard_map/ppermute | solution.py:26
  76.6 11.8 %collective-permute-start.1 = (bf16[160,1024]{1,0:T(8,128)(2,1)}, bf16[160,1024]{1,0:T(8,128)(2,1)}, u32[]{:S(2)}, u32[]{:S(2)}) collective-permute-start(bf16[160,1024]{1,0:T(8,128)(2,1)} %get-tuple-element.14), channel_id=1, source_target_pairs={{0,1},{1,2},{2,3},{3,0},{4,5},{5,6},{6,7},{7,4},{8,9},{9,10},{10,1... | collective-permute-start | bytes 983048 | tf_op jit(solution)/shard_map/ppermute | solution.py:52
  77.9 19.5 %all-to-all-start.2 = ((bf16[16,16,1024]{2,1,0:T(8,128)(2,1)}), bf16[16,16,1024]{2,1,0:T(8,128)(2,1)S(1)}, u32[]{:S(2)}, u32[]{:S(2)}) async-start(bf16[16,16,1024]{2,1,0:T(8,128)(2,1)} %bitcast.30), calls=%async_computation.2 | async-start | bytes 1048576 | tf_op jit(solution)/shard_map/all_to_all | solution.py:30
  84.3 13.1 %collective-permute-start.2 = (bf16[160,1024]{1,0:T(8,128)(2,1)}, bf16[160,1024]{1,0:T(8,128)(2,1)}, u32[]{:S(2)}, u32[]{:S(2)}) collective-permute-start(bf16[160,1024]{1,0:T(8,128)(2,1)} %get-tuple-element.14), channel_id=1, source_target_pairs={{0,2},{1,3},{2,0},{3,1},{4,6},{5,7},{6,4},{7,5},{8,10},{9,11},{10,... | collective-permute-start | bytes 983048 | tf_op jit(solution)/shard_map/ppermute | solution.py:52
  87.1 14.3 %collective-permute-start.18 = (bf16[288,640]{1,0:T(8,128)(2,1)S(1)}, bf16[288,640]{1,0:T(8,128)(2,1)S(1)}, u32[]{:S(2)}, u32[]{:S(2)}) collective-permute-start(bf16[288,640]{1,0:T(8,128)(2,1)S(1)} %collective-permute-done.14.refs_14_), channel_id=1, source_target_pairs={{0,32},{32,0},{1,33},{33,1},{2,34},{34,2},{3,35},{35,3},{4,36},{36... | collective-permute-start | bytes 1105928 | tf_op jit(solution)/shard_map/ppermute | solution.py:26
  88.4 14.7 %collective-permute-start.19 = (bf16[288,640]{1,0:T(8,128)(2,1)S(1)}, bf16[288,640]{1,0:T(8,128)(2,1)S(1)}, u32[]{:S(2)}, u32[]{:S(2)}) collective-permute-start(bf16[288,640]{1,0:T(8,128)(2,1)S(1)} %collective-permute-done.15.refs_15_), channel_id=1, source_target_pairs={{0,32},{32,0},{1,33},{33,1},{2,34},{34,2},{3,35},{35,3},{4,36},{36... | collective-permute-start | bytes 1105928 | tf_op jit(solution)/shard_map/ppermute | solution.py:26
  88.4 11.4 %collective-permute-start.3 = (bf16[160,1024]{1,0:T(8,128)(2,1)}, bf16[160,1024]{1,0:T(8,128)(2,1)S(1)}, u32[]{:S(2)}, u32[]{:S(2)}) collective-permute-start(bf16[160,1024]{1,0:T(8,128)(2,1)} %get-tuple-element.14), channel_id=1, source_target_pairs={{0,3},{1,0},{2,1},{3,2},{4,7},{5,4},{6,5},{7,6},{8,11},{9,8},{10,9... | collective-permute-start | bytes 983048 | tf_op jit(solution)/shard_map/ppermute | solution.py:52
  97.4 9.2 %collective-permute-start.20 = (bf16[288,640]{1,0:T(8,128)(2,1)}, bf16[288,640]{1,0:T(8,128)(2,1)}, u32[]{:S(2)}, u32[]{:S(2)}) collective-permute-start(bf16[288,640]{1,0:T(8,128)(2,1)} %collective-permute-done.16.refs_16_), channel_id=1, source_target_pairs={{0,32},{32,0},{1,33},{33,1},{2,34},{34,2},{3,35},{35,3},{4,36},{36... | collective-permute-start | bytes 1105928 | tf_op jit(solution)/shard_map/ppermute | solution.py:26
  99.8 23.8 %collective-permute-start.25 = (bf16[4,160,1024]{2,1,0:T(8,128)(2,1)}, bf16[4,160,1024]{2,1,0:T(8,128)(2,1)}, u32[]{:S(2)}, u32[]{:S(2)}) collective-permute-start(bf16[4,160,1024]{2,1,0:T(8,128)(2,1)} %pad_maximum_fusion.1.refs_1_), channel_id=1, source_target_pairs={{0,8},{1,9},{2,10},{3,11},{4,12},{5,13},{6,14},{7,15},{8,0},{9,1},... | collective-permute-start | bytes 3932168 | tf_op jit(solution)/shard_map/ppermute | solution.py:52
  102.2 33.1 %collective-permute-start.26 = (bf16[4,160,1024]{2,1,0:T(8,128)(2,1)}, bf16[4,160,1024]{2,1,0:T(8,128)(2,1)}, u32[]{:S(2)}, u32[]{:S(2)}) collective-permute-start(bf16[4,160,1024]{2,1,0:T(8,128)(2,1)} %pad_maximum_fusion.1.refs_1_), channel_id=1, source_target_pairs={{0,12},{1,13},{2,14},{3,15},{4,0},{5,1},{6,2},{7,3},{8,4},{9,5},{1... | collective-permute-start | bytes 3932168 | tf_op jit(solution)/shard_map/ppermute | solution.py:52
  103.8 7.0 %collective-permute-start.29 = (f32[16,1024]{1,0:T(8,128)S(1)}, f32[16,1024]{1,0:T(8,128)S(1)}, u32[]{:S(2)}, u32[]{:S(2)}) collective-permute-start(f32[16,1024]{1,0:T(8,128)S(1)} %convert_reduce_fusion), channel_id=1, source_target_pairs={{0,16},{16,0},{1,17},{17,1},{2,18},{18,2},{3,19},{19,3},{4,20},{20... | collective-permute-start | bytes 196616 | tf_op jit(solution)/shard_map/ppermute | solution.py:26
  106.6 64.2 %collective-permute-start.4 = (bf16[4,160,1024]{2,1,0:T(8,128)(2,1)}, bf16[4,160,1024]{2,1,0:T(8,128)(2,1)}, u32[]{:S(2)}, u32[]{:S(2)}) collective-permute-start(bf16[4,160,1024]{2,1,0:T(8,128)(2,1)} %pad_maximum_fusion.refs_1_), channel_id=1, source_target_pairs={{0,4},{1,5},{2,6},{3,7},{4,8},{5,9},{6,10},{7,11},{8,12},{9,13},{1... | collective-permute-start | bytes 3932168 | tf_op jit(solution)/shard_map/ppermute | solution.py:52
  110.9 59.9 %collective-permute-start.5 = (bf16[4,160,1024]{2,1,0:T(8,128)(2,1)}, bf16[4,160,1024]{2,1,0:T(8,128)(2,1)}, u32[]{:S(2)}, u32[]{:S(2)}) collective-permute-start(bf16[4,160,1024]{2,1,0:T(8,128)(2,1)} %pad_maximum_fusion.refs_1_), channel_id=1, source_target_pairs={{0,8},{1,9},{2,10},{3,11},{4,12},{5,13},{6,14},{7,15},{8,0},{9,1},... | collective-permute-start | bytes 3932168 | tf_op jit(solution)/shard_map/ppermute | solution.py:52
  111.3 59.4 %collective-permute-start.6 = (bf16[4,160,1024]{2,1,0:T(8,128)(2,1)}, bf16[4,160,1024]{2,1,0:T(8,128)(2,1)}, u32[]{:S(2)}, u32[]{:S(2)}) collective-permute-start(bf16[4,160,1024]{2,1,0:T(8,128)(2,1)} %pad_maximum_fusion.refs_1_), channel_id=1, source_target_pairs={{0,12},{1,13},{2,14},{3,15},{4,0},{5,1},{6,2},{7,3},{8,4},{9,5},{1... | collective-permute-start | bytes 3932168 | tf_op jit(solution)/shard_map/ppermute | solution.py:52
  115.5 52.0 %all-to-all-start.3 = ((bf16[16,16,1024]{2,1,0:T(8,128)(2,1)}), bf16[16,16,1024]{2,1,0:T(8,128)(2,1)}, u32[]{:S(2)}, u32[]{:S(2)}) async-start(bf16[16,16,1024]{2,1,0:T(8,128)(2,1)} %broadcast_in_dim.5), calls=%async_computation.3 | async-start | bytes 1048576 | tf_op jit(solution)/shard_map/all_to_all | solution.py:30
  (54 other events, 377.7 us)

commit v2 on v1

v2 whole, which is shorter than its diff:
```python
import jax
import jax.numpy as jnp
from jax import lax
from jax.experimental import pallas as pl
from jax.experimental.pallas import tpu as pltpu
from jax.sharding import Mesh
from jax.sharding import PartitionSpec as P

learn_rate = 0.02
beta_one = 0.9
beta_two = 0.999
epsilon = 1e-08
correct_first = 0.9999734386011124
correct_second = 0.0952078528862904

bf16 = jnp.bfloat16
f32 = jnp.float32


PLANE = ("y", "x")


def shift(value, axis, step=1):
    size = lax.axis_size(axis)
    return lax.ppermute(value, axis, [(i, (i + step) % size) for i in range(size)])


def swap(value, axes):
    return lax.all_to_all(value, axes, 0, 0, tiled=True)


def gather(block, axes):
    size = lax.axis_size(axes)
    return swap(jnp.broadcast_to(block[None], (size, *block.shape)), axes)


def around(block, axis):
    left = shift(block, axis, 1)
    right = shift(block, axis, -1)
    far = shift(block, axis, 2)
    return [block, left, far, right]


def plane_shift(value, outer, step):
    pairs = []
    for k in range(2):
        for y in range(4):
            for x in range(4):
                to_y, to_x = ((y + step) % 4, x) if (k == 0) == outer else (y, (x + step) % 4)
                pairs.append(((k * 4 + y) * 4 + x, (k * 4 + to_y) * 4 + to_x))
    return lax.ppermute(value, ("k", "y", "x"), pairs)


def plane_around(block, outer):
    left = plane_shift(block, outer, 1)
    right = plane_shift(block, outer, -1)
    far = plane_shift(block, outer, 2)
    return [block, left, far, right]


def decode(m_codes, m_exps, v_codes, v_exps):
    scale = jnp.exp2(jnp.concatenate([m_exps, v_exps], 0).astype(f32)).astype(bf16)
    codes = jnp.concatenate([m_codes, v_codes], 0).astype(f32) / 128.0
    blocks, width = scale.shape[1], codes.shape[1]
    block_of = lax.broadcasted_iota(jnp.int32, (blocks, width), 1) // (width // blocks)
    ones = (block_of == lax.broadcasted_iota(jnp.int32, (blocks, width), 0)).astype(bf16)
    return codes * mm(scale, ones)


def pair_order(mine, other, me):
    return jnp.where(me == 0, jnp.concatenate([mine, other], 0), jnp.concatenate([other, mine], 0))


def mm(a, b):
    return jnp.dot(a, b, preferred_element_type=f32)


VMEM = pl.BlockSpec(memory_space=pltpu.VMEM)
SMEM = pl.BlockSpec(memory_space=pltpu.SMEM)
HBM = pl.BlockSpec(memory_space=pltpu.HBM)


def in_hbm(values):
    return [pltpu.with_memory_space_constraint(v, pltpu.HBM) for v in values]


def ranks_as_sent(rank, own):
    take = lax.broadcasted_iota(jnp.int32, (rank, rank), 0)
    col = lax.broadcasted_iota(jnp.int32, (rank, rank), 1)
    q = lax.div(col, 2 * own)
    half = lax.rem(lax.div(col, own), 2)
    return (take == half * (rank // 2) + q * own + lax.rem(col, own)).astype(bf16)


def first_kernel(place, *refs):
    pieces, xs, proj = refs[:4], refs[4:12], refs[12]
    acc, low, xt, w, xb, pb, wsem, xsem, psem = refs[13:]
    rows = pieces[0].shape[1]
    feat = xt.shape[2]
    h, k, z, y, x = (place[i] for i in range(5))

    def w_copy(src, to_y, to_x):
        at = pl.ds(pl.multiple_of(to_y * feat + to_x * rows, 32), rows)
        return pltpu.make_async_copy(src, w.at[at], wsem.at[to_y, to_x])

    def x_copy(src, side, chunk):
        to = pl.ds(pl.multiple_of(chunk * feat, 128), feat)
        return pltpu.make_async_copy(src, xb.at[side, :, to], xsem.at[side, chunk])

    def p_copy(side):
        half_h = jnp.where(side == 0, h, 1 - h)
        return pltpu.make_async_copy(proj.at[half_h], pb.at[side], psem.at[side])

    for s in range(4):
        from_z = lax.rem(z - s + 4, 4)
        side = jnp.where(from_z // 2 == h, 0, 1)
        x_copy(xs[s], side, 2 * lax.rem(from_z, 2) + k).start()
        x_copy(xs[4 + s], side, 2 * lax.rem(from_z, 2) + 1 - k).start()
    for s in range(4):
        for t in range(4):
            back_y = jnp.where(k == 0, s, t)
            back_x = jnp.where(k == 0, t, s)
            w_copy(pieces[s].at[t], lax.rem(y - back_y + 4, 4), lax.rem(x - back_x + 4, 4)).start()
    for i in range(2):
        p_copy(i).start()

    for i in range(2):
        for j in range(4):
            x_copy(xs[0], i, j).wait()

    @pl.when(k == 0)
    def _():
        for c in range(4):
            xt[c] = xb[1, :, c * feat : (c + 1) * feat]

    @pl.when(k == 1)
    def _():
        for c in range(4):
            xt[c] = jnp.concatenate(
                [xb[1, :, j * feat + c * rows : j * feat + (c + 1) * rows] for j in range(4)], axis=1
            )

    for i in range(2):
        for j in (2 * i, 2 * i + 1):
            for t in range(4):
                w_copy(pieces[0].at[0], j, t).wait()
        at = slice(2 * i * feat, 2 * (i + 1) * feat)
        part = mm(xb[0, :, at], w[at])
        total = part if i == 0 else total + part
    acc[...] = total
    for i in range(2):
        p_copy(i).wait()
    total_low = (mm(xb[0], pb[0]) + mm(xb[1], pb[1])).astype(bf16)
    low[...] = mm(total_low, ranks_as_sent(total_low.shape[1], 8)).astype(bf16)


def first_side(place, pieces, xs, proj):
    _, _, width = pieces[0].shape
    tok, feat = xs[0].shape
    rank = proj.shape[-1]
    shapes = [((tok, width), f32), ((tok, rank), bf16), ((4, tok, feat), bf16)]
    return pl.pallas_call(
        first_kernel,
        in_specs=[SMEM, *[HBM] * 13],
        out_specs=[VMEM] * 3,
        out_shape=[jax.ShapeDtypeStruct(*s) for s in shapes],
        scratch_shapes=[
            pltpu.VMEM((4 * feat, width), bf16),
            pltpu.VMEM((2, tok, 4 * feat), bf16),
            pltpu.VMEM((2, 4 * feat, rank), bf16),
            pltpu.SemaphoreType.DMA((4, 4)),
            pltpu.SemaphoreType.DMA((2, 4)),
            pltpu.SemaphoreType.DMA((2,)),
        ],
        compiler_params=pltpu.CompilerParams(vmem_limit_bytes=32 << 20),
        name="first_product",
    )(place, *in_hbm([*pieces, *xs, proj]))


def add_pieces(place, pieces, steps, xt, w, sem, total):
    rows = pieces[0].shape[1]
    k, y, x = (place[i] for i in (1, 3, 4))
    outer = jnp.where(k == 0, y, x)
    inner = jnp.where(k == 0, x, y)

    def w_copy(src, n, to):
        at = pl.ds(pl.multiple_of(to * rows, 32), rows)
        return pltpu.make_async_copy(src, w.at[n, at], sem.at[n, to])

    for n, piece in enumerate(pieces):
        for t in range(4):
            w_copy(piece.at[t], n, lax.rem(inner - t + 4, 4)).start()
    total = total()
    for n, (piece, s) in enumerate(zip(pieces, steps)):
        for t in range(4):
            w_copy(piece.at[0], n, t).wait()
        total = total + mm(xt[lax.rem(outer - s + 4, 4)], w[n])
    return total


def middle_kernel(place, a, b, c, xt, acc, out, w, sem):
    out[...] = add_pieces(place, (a, b, c), (0, 1, 3), xt, w, sem, lambda: acc[...])


def middle_side(place, pieces, xt, acc):
    count, rows, width = pieces[0].shape
    return pl.pallas_call(
        middle_kernel,
        in_specs=[SMEM, *[HBM] * 3, VMEM, VMEM],
        out_specs=VMEM,
        out_shape=jax.ShapeDtypeStruct(acc.shape, f32),
        scratch_shapes=[pltpu.VMEM((3, count * rows, width), bf16), pltpu.SemaphoreType.DMA((3, 4))],
        compiler_params=pltpu.CompilerParams(vmem_limit_bytes=32 << 20),
        name="middle_product",
    )(place, *in_hbm(pieces), xt, acc)


def last_kernel(place, far, proj, xt, acc, low, direction, weight, out, new_weight, w, pb, sem, psem):
    rows, width = weight.shape
    rank = low.shape[1]
    at = pl.ds(pl.multiple_of(place[5] * rows, 32), rows)
    p_copy = pltpu.make_async_copy(proj.at[at], pb, psem)
    p_copy.start()
    turned = direction[...].reshape(rank, width)

    def start():
        p_copy.wait()
        p_rows = mm(pb[...], ranks_as_sent(rank, 8)).astype(bf16)
        new_weight[...] = (weight[...].astype(f32) - learn_rate * mm(p_rows, turned)).astype(bf16)
        return acc[...] - learn_rate * mm(low[...], turned)

    out[...] = add_pieces(place, (far,), (2,), xt, w, sem, start).astype(bf16)


def last_side(place, far, proj, xt, acc, low, direction, weight):
    count, rows, width = far.shape
    return pl.pallas_call(
        last_kernel,
        in_specs=[SMEM, HBM, HBM, *[VMEM] * 5],
        out_specs=[VMEM, VMEM],
        out_shape=[jax.ShapeDtypeStruct(acc.shape, bf16), jax.ShapeDtypeStruct(weight.shape, bf16)],
        scratch_shapes=[
            pltpu.VMEM((1, count * rows, width), bf16),
            pltpu.VMEM((rows, proj.shape[1]), bf16),
            pltpu.SemaphoreType.DMA((1, 4)),
            pltpu.SemaphoreType.DMA,
        ],
        compiler_params=pltpu.CompilerParams(vmem_limit_bytes=32 << 20),
        name="last_product",
    )(place, *in_hbm([far, proj]), xt, acc, low, direction, weight)


def body(acts, out_grad, projection, weight, m_codes, m_exps, v_codes, v_exps, next_acts):
    k = lax.axis_index("k")
    z = lax.axis_index("z")
    h = lax.axis_index("h")
    tok, feat = acts.shape
    half = tok // 2
    rank = projection.shape[1]
    _, width = weight.shape
    tokens_all = tok * lax.axis_size(("h", "y", "x"))

    mine = lax.dynamic_slice_in_dim(acts, k * half, half, 0)
    theirs = lax.dynamic_slice_in_dim(acts, (1 - k) * half, half, 0)
    got = shift(theirs, "k")
    p_mine = lax.dynamic_slice_in_dim(projection, (2 * z + k) * feat, feat, 0)
    p_got = lax.dynamic_slice_in_dim(projection, (2 * z + 1 - k) * feat, feat, 0)
    part = mm(mine, p_mine) + mm(got, p_got)
    low = swap(part.reshape(4, half // 4, rank), "z").sum(axis=0).astype(bf16)
    low = gather(low, "z").reshape(half, rank)
    lowrank = pair_order(low, shift(low, "k"), k)

    grad_part = lax.dot_general(lowrank, out_grad, (((0,), (0,)), ((), ())), preferred_element_type=f32)
    q = lax.axis_size(PLANE)
    own = rank // q // 2
    cut = grad_part.astype(bf16).reshape(2, q, own, width).transpose(1, 0, 2, 3).reshape(q, 2 * own, width)
    plane = swap(cut, PLANE).astype(f32).sum(axis=0)
    moments = decode(m_codes, m_exps, v_codes, v_exps)
    other = shift(jnp.concatenate([plane, moments], 0), "h")
    grad = (plane + other[: 2 * own]) / tokens_all
    other = other[2 * own :]
    shard = (weight, shift(weight, "h"))
    m_old = pair_order(moments[:own], other[:own], h)
    v_old = pair_order(moments[own:], other[own:], h)
    first = beta_one * m_old + (1.0 - beta_one) * grad
    second = beta_two * v_old + (1.0 - beta_two) * grad * grad
    both = first / correct_first / (jnp.sqrt(second / correct_second) + epsilon)
    update = jnp.where(h == 0, both[:own], both[own:])
    direction = gather(both.astype(bf16), PLANE)

    xs = around(next_acts, "z")
    xs = [*xs, *(shift(piece, "k") for piece in xs)]

    sides = []
    for s in (0, 1):
        block = plane_around(shard[s], False)
        block = jnp.stack(block)
        sides.append(plane_around(block, True))
    place = [h, k, z, lax.axis_index("y"), lax.axis_index("x"), lax.axis_index(("h", "y", "x"))]
    place = jnp.stack(place).astype(jnp.int32)
    acc, next_low, xt = first_side(place, sides[0], xs, projection.reshape(2, 4 * feat, rank))
    mine_w, left, far, right = sides[1]
    acc = middle_side(place, [mine_w, left, right], xt, acc)
    out, new_weight = last_side(place, far, projection, xt, acc, next_low, direction, weight)
    return (out, new_weight, update)


def solution(mesh):
    torus = Mesh(mesh.devices.reshape(mesh.shape["col"] // 2, 2, 2, 4, 4), ("z", "k", "h", "y", "x"))
    both = P(("h", "y", "x"), ("z", "k"))
    return jax.shard_map(
        body,
        mesh=torus,
        in_specs=(both, both, P(), both, both, both, both, both, both),
        out_specs=(both, both, both),
        check_vma=False,
    )
```

time: 192 us -> 181 us (0.943)
  the two profiles are of different devices: /device:TPU:195 before, /device:TPU:1 now
where the time goes in v2:
time: 181 us; the launch traced here: 180 us
  starting transfers between devices  90.4 us (50%)
  waiting for transfers between devices  51.9 us (29%)
  Pallas kernels  19.3 us (11%)
  local copies, waits for them, and re-layouts  7.09 us (4%)
  other arithmetic  5.45 us (3%)
  matrix products  5.23 us (3%)
    ppermute x12, starting transfers between devices, plane_shift(): return lax.ppermute(value, ('k', 'y', 'x'), pairs)  47.3 us
    ppermute x12, waiting for transfers between devices, plane_shift(): return lax.ppermute(value, ('k', 'y', 'x'), pairs)  41.3 us
    ppermute x11, starting transfers between devices, shift(): lax.ppermute(value, axis, [(i, (i + step) % size) for i in range(size)])  21.7 us
    all_to_all x4, starting transfers between devices, swap(): return lax.all_to_all(value, axes, 0, 0, tiled=True)  21.3 us
    pallas_call x1, Pallas kernels, first_side(): pl.pallas_call(first_kernel, in_specs=[SMEM, *[HBM] * 13], out_specs=[VME...  11.1 us
    all_to_all x4, waiting for transfers between devices, swap(): return lax.all_to_all(value, axes, 0, 0, tiled=True)  7.68 us
    dot_general x3, matrix products, mm(): return jnp.dot(a, b, preferred_element_type=f32)  4.78 us
    pallas_call x1, Pallas kernels, last_side(): pl.pallas_call(last_kernel, in_specs=[SMEM, HBM, HBM, *[VMEM] * 5], out_s...  4.09 us
  transfers between devices with their start and end apart: 27, of which 7 were waited for; matrix products, arithmetic and copies ran while one was open for 7% of the time, Pallas kernels for 8%

profile of v2, /device:TPU:1, one launch (start us, length us, event | category | flops | bytes accessed | tf_op | source)
XLA Modules:
  0.0 180.5 jit_solution(5990198545503176186)
XLA Ops:
  1.8 3.3 %collective-permute-start.20 = (bf16[192,640]{1,0:T(8,128)(2,1)S(1)}, bf16[192,640]{1,0:T(8,128)(2,1)S(1)}, u32[]{:S(2)}, u32[]{:S(2)}) collective-permute-start(bf16[192,640]{1,0:T(8,128)(2,1)S(1)} %constant_dynamic-slice_fusion), channel_id=1, source_target_pairs={{0,32},{32,0},{1,33},{33,1},{2,34},{34,2},{3,35},{35,3},{4,36},{36... | collective-permute-start | bytes 737288 | tf_op jit(solution)/shard_map/ppermute | solution.py:25
  5.1 2.2 %collective-permute-start.6 = (bf16[160,1024]{1,0:T(8,128)(2,1)}, bf16[160,1024]{1,0:T(8,128)(2,1)}, u32[]{:S(2)}, u32[]{:S(2)}) collective-permute-start(bf16[160,1024]{1,0:T(8,128)(2,1)} %weight.1), channel_id=1, source_target_pairs={{0,2},{1,3},{2,0},{3,1},{4,6},{5,7},{6,4},{7,5},{8,10},{9,11},{10,... | collective-permute-start | bytes 983048 | tf_op jit(solution)/shard_map/ppermute | solution.py:51
  8.3 1.3 fusion.1
  9.7 1.9 %convolution_add_fusion = f32[192,256]{1,0:T(8,128)} fusion(f32[192,256]{1,0:T(8,128)S(1)} %fusion.1, bf16[192,640]{1,0:T(8,128)(2,1)S(1)} %collective-permute-done.20, bf16[5120,256]{1,0:T(8,128)(2,1)} %proj.1, s32[]{:T(128)S(6)} %select_n.51), kind=kOutput, calls=%fused_computation.3 | convolution fusion | flops 62963712 | bytes 966660 | tf_op jit(solution)/shard_map/dot_general | solution.py:75
  11.6 5.6 %all-to-all-start = ((f32[4,48,256]{2,1,0:T(8,128)}), f32[4,48,256]{2,1,0:T(8,128)S(1)}, u32[]{:S(2)}, u32[]{:S(2)}) async-start(f32[4,48,256]{2,1,0:T(8,128)} %bitcast.15), calls=%async_computation | async-start | bytes 393216 | tf_op jit(solution)/shard_map/all_to_all | solution.py:29
  17.2 1.5 collective-permute-start.11
  18.7 2.1 %collective-permute-start.12 = (bf16[384,640]{1,0:T(8,128)(2,1)S(1)}, bf16[384,640]{1,0:T(8,128)(2,1)}, u32[]{:S(2)}, u32[]{:S(2)}) collective-permute-start(bf16[384,640]{1,0:T(8,128)(2,1)S(1)} %copy-done.6), channel_id=1, source_target_pairs={{0,128},{64,192},{128,0},{192,64},{1,129},{65,193},{129,1},{193,65... | collective-permute-start | bytes 1474568 | tf_op jit(solution)/shard_map/ppermute | solution.py:25
  20.8 4.7 %collective-permute-start = (bf16[160,1024]{1,0:T(8,128)(2,1)S(1)}, bf16[160,1024]{1,0:T(8,128)(2,1)S(1)}, u32[]{:S(2)}, u32[]{:S(2)}) collective-permute-start(bf16[160,1024]{1,0:T(8,128)(2,1)S(1)} %copy-done.3), channel_id=1, source_target_pairs={{0,16},{16,0},{1,17},{17,1},{2,18},{18,2},{3,19},{19,3},{4,20},{20... | collective-permute-start | bytes 983048 | tf_op jit(solution)/shard_map/ppermute | solution.py:25
  26.2 3.3 %all-to-all-start.1 = ((bf16[4,48,256]{2,1,0:T(8,128)(2,1)}), bf16[4,48,256]{2,1,0:T(8,128)(2,1)S(1)}, u32[]{:S(2)}, u32[]{:S(2)}) async-start(bf16[4,48,256]{2,1,0:T(8,128)(2,1)} %broadcast_in_dim.4), calls=%async_computation.1 | async-start | bytes 196608 | tf_op jit(solution)/shard_map/all_to_all | solution.py:29
  29.5 1.3 pad_maximum_fusion.1.refs_0_
  30.8 37.7 %collective-permute-start.10 = (bf16[4,160,1024]{2,1,0:T(8,128)(2,1)S(1)}, bf16[4,160,1024]{2,1,0:T(8,128)(2,1)}, u32[]{:S(2)}, u32[]{:S(2)}) collective-permute-start(bf16[4,160,1024]{2,1,0:T(8,128)(2,1)S(1)} %pad_maximum_fusion.1.refs_0_), channel_id=1, source_target_pairs={{0,12},{1,13},{2,14},{3,15},{4,0},{5,1},{6,2},{7,3},{8,4},{9,5},{1... | collective-permute-start | bytes 3932168 | tf_op jit(solution)/shard_map/ppermute | solution.py:51
  68.5 3.0 %all-to-all-done.1 = bf16[4,48,256]{2,1,0:T(8,128)(2,1)S(1)} async-done(((bf16[4,48,256]{2,1,0:T(8,128)(2,1)}), bf16[4,48,256]{2,1,0:T(8,128)(2,1)S(1)}, u32[]{:S(2)}, u32[]{:S(2)}) %all-to-all-start.1) | async-done | bytes 98336 | tf_op jit(solution)/shard_map/all_to_all | solution.py:29
  71.6 1.8 collective-permute-start.21
  73.4 1.2 collective-permute-start.13
  77.4 5.9 %all-to-all-start.2 = ((bf16[16,16,1024]{2,1,0:T(8,128)(2,1)}), bf16[16,16,1024]{2,1,0:T(8,128)(2,1)S(1)}, u32[]{:S(2)}, u32[]{:S(2)}) async-start(bf16[16,16,1024]{2,1,0:T(8,128)(2,1)} %bitcast.24), calls=%async_computation.2 | async-start | bytes 1048576 | tf_op jit(solution)/shard_map/all_to_all | solution.py:29
  83.3 2.9 %collective-permute-done.13.refs_7_ = bf16[384,640]{1,0:T(8,128)(2,1)} collective-permute-done((bf16[384,640]{1,0:T(8,128)(2,1)S(1)}, bf16[384,640]{1,0:T(8,128)(2,1)}, u32[]{:S(2)}, u32[]{:S(2)}) %collective-permute-start.13) | collective-permute-done | bytes 491552 | tf_op jit(solution)/shard_map/ppermute | solution.py:25
  86.3 1.7 collective-permute-start.15
  88.6 1.5 convolution_multiply_fusion
  90.1 4.6 %all-to-all-done.2 = bf16[16,16,1024]{2,1,0:T(8,128)(2,1)S(1)} async-done(((bf16[16,16,1024]{2,1,0:T(8,128)(2,1)}), bf16[16,16,1024]{2,1,0:T(8,128)(2,1)S(1)}, u32[]{:S(2)}, u32[]{:S(2)}) %all-to-all-start.2) | async-done | bytes 524320 | tf_op jit(solution)/shard_map/all_to_all | solution.py:29
  95.7 1.7 collective-permute-done.3
  97.4 4.7 %collective-permute-start.22 = (f32[32,1024]{1,0:T(8,128)S(1)}, f32[32,1024]{1,0:T(8,128)S(1)}, u32[]{:S(2)}, u32[]{:S(2)}) collective-permute-start(f32[32,1024]{1,0:T(8,128)S(1)} %pad_maximum_fusion.2), channel_id=1, source_target_pairs={{0,16},{16,0},{1,17},{17,1},{2,18},{18,2},{3,19},{19,3},{4,20},{20... | collective-permute-start | bytes 393224 | tf_op jit(solution)/shard_map/ppermute | solution.py:25
  102.0 2.5 %pad_maximum_fusion.a = bf16[4,160,1024]{2,1,0:T(8,128)(2,1)} fusion(bf16[1,160,1024]{2,1,0:T(8,128)(2,1)} %bitcast.9, bf16[1,160,1024]{2,1,0:T(8,128)(2,1)} %bitcast.8, bf16[1,160,1024]{2,1,0:T(8,128)(2,1)} %bitcast.7, bf16[1,160,1024]{2,1,0:T(8,128)(2,1)S(1)} %bitcast.28), kind=kLoop, calls=%fused_computation | loop fusion | flops 1966080 | bytes 2621440 | tf_op jit(solution)/shard_map/stack | solution.py:297
  105.0 1.6 collective-permute-start.9
  107.8 1.5 collective-permute-start.19
  110.6 6.5 %all-to-all-start.3 = ((bf16[16,16,1024]{2,1,0:T(8,128)(2,1)}), bf16[16,16,1024]{2,1,0:T(8,128)(2,1)S(1)}, u32[]{:S(2)}, u32[]{:S(2)}) async-start(bf16[16,16,1024]{2,1,0:T(8,128)(2,1)} %broadcast_in_dim.5), calls=%async_computation.3 | async-start | bytes 1048576 | tf_op jit(solution)/shard_map/all_to_all | solution.py:29
  117.8 10.4 %collective-permute-done.8.refs_1_ = bf16[4,160,1024]{2,1,0:T(8,128)(2,1)} collective-permute-done((bf16[4,160,1024]{2,1,0:T(8,128)(2,1)S(1)}, bf16[4,160,1024]{2,1,0:T(8,128)(2,1)}, u32[]{:S(2)}, u32[]{:S(2)}) %collective-permute-start.8) | collective-permute-done | bytes 1310752 | tf_op jit(solution)/shard_map/ppermute | solution.py:51
  128.3 10.7 %collective-permute-done.9.refs_2_ = bf16[4,160,1024]{2,1,0:T(8,128)(2,1)} collective-permute-done((bf16[4,160,1024]{2,1,0:T(8,128)(2,1)S(1)}, bf16[4,160,1024]{2,1,0:T(8,128)(2,1)}, u32[]{:S(2)}, u32[]{:S(2)}) %collective-permute-start.9) | collective-permute-done | bytes 1310752 | tf_op jit(solution)/shard_map/ppermute | solution.py:51
  138.9 11.1 %first_product.1 = (f32[384,1024]{1,0:T(8,128)S(1)}, bf16[384,256]{1,0:T(8,128)(2,1)S(1)}, bf16[4,384,640]{2,1,0:T(8,128)(2,1)S(1)}) custom-call(s32[6]{0:T(128)S(1)} %stack.57.place, bf16[4,160,1024]{2,1,0:T(8,128)(2,1)} %copy-done.5, bf16[4,160,1024]{2,1,0:T(8,128)(2,1)} %collective-permute-done.8.refs_1_, ...), custom_call_target="tpu_custom_call" | custom-call | tf_op jit(solution)/shard_map/first_product/pallas_call | solution.py:162
  150.1 18.5 %collective-permute-done.18.b = bf16[4,160,1024]{2,1,0:T(8,128)(2,1)} collective-permute-done((bf16[4,160,1024]{2,1,0:T(8,128)(2,1)}, bf16[4,160,1024]{2,1,0:T(8,128)(2,1)}, u32[]{:S(2)}, u32[]{:S(2)}) %collective-permute-start.18) | collective-permute-done | bytes 1310752 | tf_op jit(solution)/shard_map/ppermute | solution.py:51
  168.6 4.1 %middle_product.1.acc = f32[384,1024]{1,0:T(8,128)S(1)} custom-call(s32[6]{0:T(128)S(1)} %stack.57.place, bf16[4,160,1024]{2,1,0:T(8,128)(2,1)} %pad_maximum_fusion.a, bf16[4,160,1024]{2,1,0:T(8,128)(2,1)} %collective-permute-done.18.b, bf16[4,160,1024]{2,1,0:T(8,128)(2,1)} %collective-permute-done.19.c, bf16[4,384,640]{2,1,0:T(8,128)(2,1)S(1)} %get-tuple-element.8.xt, ...), custom_call_target="tpu_custom_call" | custom-call | tf_op jit(solution)/shard_map/middle_product/pallas_call | solution.py:207
  173.8 1.4 copy-done.2
  176.2 4.1 %last_product.1 = (bf16[384,1024]{1,0:T(8,128)(2,1)}, bf16[160,1024]{1,0:T(8,128)(2,1)}) custom-call(s32[6]{0:T(128)S(1)} %stack.57.place, bf16[4,160,1024]{2,1,0:T(8,128)(2,1)} %collective-permute-done.4.far, bf16[5120,256]{1,0:T(8,128)(2,1)} %proj.1, bf16[4,384,640]{2,1,0:T(8,128)(2,1)S(1)} %get-tuple-element.8.xt, f32[384,1024]{1,0:T(8,128)S(1)} %copy-done.2, ...), custom_call_target="tpu_custom_call" | custom-call | tf_op jit(solution)/shard_map/last_product/pallas_call | solution.py:237
  (71 shorter events, 12.9 us)
Async XLA Ops:
  0.6 75.4 %copy-start = (bf16[384,1024]{1,0:T(8,128)(2,1)S(1)}, bf16[384,1024]{1,0:T(8,128)(2,1)}, u32[]{:S(2)}) copy-start(bf16[384,1024]{1,0:T(8,128)(2,1)} %param.10) | copy-start | bytes 2359300
  0.7 16.6 %copy-start.6 = (bf16[384,640]{1,0:T(8,128)(2,1)S(1)}, bf16[384,640]{1,0:T(8,128)(2,1)}, u32[]{:S(2)}) copy-start(bf16[384,640]{1,0:T(8,128)(2,1)} %refs_4_.1) | copy-start | bytes 1474564
  0.7 20.1 %copy-start.3 = (bf16[160,1024]{1,0:T(8,128)(2,1)S(1)}, bf16[160,1024]{1,0:T(8,128)(2,1)}, u32[]{:S(2)}) copy-start(bf16[160,1024]{1,0:T(8,128)(2,1)} %weight.1) | copy-start | bytes 983044
  1.8 7.9 %collective-permute-start.20 = (bf16[192,640]{1,0:T(8,128)(2,1)S(1)}, bf16[192,640]{1,0:T(8,128)(2,1)S(1)}, u32[]{:S(2)}, u32[]{:S(2)}) collective-permute-start(bf16[192,640]{1,0:T(8,128)(2,1)S(1)} %constant_dynamic-slice_fusion), channel_id=1, source_target_pairs={{0,32},{32,0},{1,33},{33,1},{2,34},{34,2},{3,35},{35,3},{4,36},{36... | collective-permute-start | bytes 737288 | tf_op jit(solution)/shard_map/ppermute | solution.py:25
  5.1 15.7 %collective-permute-start.5 = (bf16[160,1024]{1,0:T(8,128)(2,1)}, bf16[160,1024]{1,0:T(8,128)(2,1)S(1)}, u32[]{:S(2)}, u32[]{:S(2)}) collective-permute-start(bf16[160,1024]{1,0:T(8,128)(2,1)} %weight.1), channel_id=1, source_target_pairs={{0,1},{1,2},{2,3},{3,0},{4,5},{5,6},{6,7},{7,4},{8,9},{9,10},{10,1... | collective-permute-start | bytes 983048 | tf_op jit(solution)/shard_map/ppermute | solution.py:51
  5.1 24.4 %collective-permute-start.6 = (bf16[160,1024]{1,0:T(8,128)(2,1)}, bf16[160,1024]{1,0:T(8,128)(2,1)}, u32[]{:S(2)}, u32[]{:S(2)}) collective-permute-start(bf16[160,1024]{1,0:T(8,128)(2,1)} %weight.1), channel_id=1, source_target_pairs={{0,2},{1,3},{2,0},{3,1},{4,6},{5,7},{6,4},{7,5},{8,10},{9,11},{10,... | collective-permute-start | bytes 983048 | tf_op jit(solution)/shard_map/ppermute | solution.py:51
  7.3 22.2 %collective-permute-start.7 = (bf16[160,1024]{1,0:T(8,128)(2,1)}, bf16[160,1024]{1,0:T(8,128)(2,1)}, u32[]{:S(2)}, u32[]{:S(2)}) collective-permute-start(bf16[160,1024]{1,0:T(8,128)(2,1)} %weight.1), channel_id=1, source_target_pairs={{0,3},{1,0},{2,1},{3,2},{4,7},{5,4},{6,5},{7,6},{8,11},{9,8},{10,9... | collective-permute-start | bytes 983048 | tf_op jit(solution)/shard_map/ppermute | solution.py:51
  11.6 13.9 %all-to-all-start = ((f32[4,48,256]{2,1,0:T(8,128)}), f32[4,48,256]{2,1,0:T(8,128)S(1)}, u32[]{:S(2)}, u32[]{:S(2)}) async-start(f32[4,48,256]{2,1,0:T(8,128)} %bitcast.15), calls=%async_computation | async-start | bytes 393216 | tf_op jit(solution)/shard_map/all_to_all | solution.py:29
  17.2 57.4 %collective-permute-start.11 = (bf16[384,640]{1,0:T(8,128)(2,1)S(1)}, bf16[384,640]{1,0:T(8,128)(2,1)}, u32[]{:S(2)}, u32[]{:S(2)}) collective-permute-start(bf16[384,640]{1,0:T(8,128)(2,1)S(1)} %copy-done.6), channel_id=1, source_target_pairs={{0,64},{64,128},{128,192},{192,0},{1,65},{65,129},{129,193},{193,1... | collective-permute-start | bytes 1474568 | tf_op jit(solution)/shard_map/ppermute | solution.py:25
  18.7 56.2 %collective-permute-start.12 = (bf16[384,640]{1,0:T(8,128)(2,1)S(1)}, bf16[384,640]{1,0:T(8,128)(2,1)}, u32[]{:S(2)}, u32[]{:S(2)}) collective-permute-start(bf16[384,640]{1,0:T(8,128)(2,1)S(1)} %copy-done.6), channel_id=1, source_target_pairs={{0,128},{64,192},{128,0},{192,64},{1,129},{65,193},{129,1},{193,65... | collective-permute-start | bytes 1474568 | tf_op jit(solution)/shard_map/ppermute | solution.py:25
  20.8 52.6 %collective-permute-start = (bf16[160,1024]{1,0:T(8,128)(2,1)S(1)}, bf16[160,1024]{1,0:T(8,128)(2,1)S(1)}, u32[]{:S(2)}, u32[]{:S(2)}) collective-permute-start(bf16[160,1024]{1,0:T(8,128)(2,1)S(1)} %copy-done.3), channel_id=1, source_target_pairs={{0,16},{16,0},{1,17},{17,1},{2,18},{18,2},{3,19},{19,3},{4,20},{20... | collective-permute-start | bytes 983048 | tf_op jit(solution)/shard_map/ppermute | solution.py:25
  26.2 45.4 %all-to-all-start.1 = ((bf16[4,48,256]{2,1,0:T(8,128)(2,1)}), bf16[4,48,256]{2,1,0:T(8,128)(2,1)S(1)}, u32[]{:S(2)}, u32[]{:S(2)}) async-start(bf16[4,48,256]{2,1,0:T(8,128)(2,1)} %broadcast_in_dim.4), calls=%async_computation.1 | async-start | bytes 196608 | tf_op jit(solution)/shard_map/all_to_all | solution.py:29
  30.8 74.2 %copy-start.5 = (bf16[4,160,1024]{2,1,0:T(8,128)(2,1)}, bf16[4,160,1024]{2,1,0:T(8,128)(2,1)S(1)}, u32[]{:S(2)}) copy-start(bf16[4,160,1024]{2,1,0:T(8,128)(2,1)S(1)} %pad_maximum_fusion.1.refs_0_) | copy-start | bytes 3932164
  30.8 78.5 %collective-permute-start.10 = (bf16[4,160,1024]{2,1,0:T(8,128)(2,1)S(1)}, bf16[4,160,1024]{2,1,0:T(8,128)(2,1)}, u32[]{:S(2)}, u32[]{:S(2)}) collective-permute-start(bf16[4,160,1024]{2,1,0:T(8,128)(2,1)S(1)} %pad_maximum_fusion.1.refs_0_), channel_id=1, source_target_pairs={{0,12},{1,13},{2,14},{3,15},{4,0},{5,1},{6,2},{7,3},{8,4},{9,5},{1... | collective-permute-start | bytes 3932168 | tf_op jit(solution)/shard_map/ppermute | solution.py:51
  71.6 3.7 %collective-permute-start.21 = (bf16[192,256]{1,0:T(8,128)(2,1)S(1)}, bf16[192,256]{1,0:T(8,128)(2,1)S(1)}, u32[]{:S(2)}, u32[]{:S(2)}) collective-permute-start(bf16[192,256]{1,0:T(8,128)(2,1)S(1)} %bitcast.30), channel_id=1, source_target_pairs={{0,32},{32,0},{1,33},{33,1},{2,34},{34,2},{3,35},{35,3},{4,36},{36... | collective-permute-start | bytes 294920 | tf_op jit(solution)/shard_map/ppermute | solution.py:25
  73.4 12.9 %collective-permute-start.13 = (bf16[384,640]{1,0:T(8,128)(2,1)S(1)}, bf16[384,640]{1,0:T(8,128)(2,1)}, u32[]{:S(2)}, u32[]{:S(2)}) collective-permute-start(bf16[384,640]{1,0:T(8,128)(2,1)S(1)} %copy-done.6), channel_id=1, source_target_pairs={{0,192},{64,0},{128,64},{192,128},{1,193},{65,1},{129,65},{193,129... | collective-permute-start | bytes 1474568 | tf_op jit(solution)/shard_map/ppermute | solution.py:25
  74.6 11.7 %collective-permute-start.14 = (bf16[384,640]{1,0:T(8,128)(2,1)S(1)}, bf16[384,640]{1,0:T(8,128)(2,1)}, u32[]{:S(2)}, u32[]{:S(2)}) collective-permute-start(bf16[384,640]{1,0:T(8,128)(2,1)S(1)} %copy-done.6), channel_id=1, source_target_pairs={{0,32},{32,0},{1,33},{33,1},{2,34},{34,2},{3,35},{35,3},{4,36},{36... | collective-permute-start | bytes 1474568 | tf_op jit(solution)/shard_map/ppermute | solution.py:25
  74.9 13.2 %collective-permute-start.1 = (bf16[160,1024]{1,0:T(8,128)(2,1)S(1)}, bf16[160,1024]{1,0:T(8,128)(2,1)}, u32[]{:S(2)}, u32[]{:S(2)}) collective-permute-start(bf16[160,1024]{1,0:T(8,128)(2,1)S(1)} %collective-permute-done), channel_id=1, source_target_pairs={{0,1},{1,2},{2,3},{3,0},{4,5},{5,6},{6,7},{7,4},{8,9},{9,10},{10,1... | collective-permute-start | bytes 983048 | tf_op jit(solution)/shard_map/ppermute | solution.py:51
  75.3 12.9 %collective-permute-start.2 = (bf16[160,1024]{1,0:T(8,128)(2,1)S(1)}, bf16[160,1024]{1,0:T(8,128)(2,1)}, u32[]{:S(2)}, u32[]{:S(2)}) collective-permute-start(bf16[160,1024]{1,0:T(8,128)(2,1)S(1)} %collective-permute-done), channel_id=1, source_target_pairs={{0,2},{1,3},{2,0},{3,1},{4,6},{5,7},{6,4},{7,5},{8,10},{9,11},{10,... | collective-permute-start | bytes 983048 | tf_op jit(solution)/shard_map/ppermute | solution.py:51
  77.4 17.3 %all-to-all-start.2 = ((bf16[16,16,1024]{2,1,0:T(8,128)(2,1)}), bf16[16,16,1024]{2,1,0:T(8,128)(2,1)S(1)}, u32[]{:S(2)}, u32[]{:S(2)}) async-start(bf16[16,16,1024]{2,1,0:T(8,128)(2,1)} %bitcast.24), calls=%async_computation.2 | async-start | bytes 1048576 | tf_op jit(solution)/shard_map/all_to_all | solution.py:29
  86.3 11.1 %collective-permute-start.3 = (bf16[160,1024]{1,0:T(8,128)(2,1)S(1)}, bf16[160,1024]{1,0:T(8,128)(2,1)}, u32[]{:S(2)}, u32[]{:S(2)}) collective-permute-start(bf16[160,1024]{1,0:T(8,128)(2,1)S(1)} %collective-permute-done), channel_id=1, source_target_pairs={{0,3},{1,0},{2,1},{3,2},{4,7},{5,4},{6,5},{7,6},{8,11},{9,8},{10,9... | collective-permute-start | bytes 983048 | tf_op jit(solution)/shard_map/ppermute | solution.py:51
  86.3 18.2 %collective-permute-start.15 = (bf16[384,640]{1,0:T(8,128)(2,1)}, bf16[384,640]{1,0:T(8,128)(2,1)S(1)}, u32[]{:S(2)}, u32[]{:S(2)}) collective-permute-start(bf16[384,640]{1,0:T(8,128)(2,1)} %collective-permute-done.11.refs_5_), channel_id=1, source_target_pairs={{0,32},{32,0},{1,33},{33,1},{2,34},{34,2},{3,35},{35,3},{4,36},{36... | collective-permute-start | bytes 1474568 | tf_op jit(solution)/shard_map/ppermute | solution.py:25
  88.0 17.0 %collective-permute-start.16 = (bf16[384,640]{1,0:T(8,128)(2,1)}, bf16[384,640]{1,0:T(8,128)(2,1)}, u32[]{:S(2)}, u32[]{:S(2)}) collective-permute-start(bf16[384,640]{1,0:T(8,128)(2,1)} %collective-permute-done.12.refs_6_), channel_id=1, source_target_pairs={{0,32},{32,0},{1,33},{33,1},{2,34},{34,2},{3,35},{35,3},{4,36},{36... | collective-permute-start | bytes 1474568 | tf_op jit(solution)/shard_map/ppermute | solution.py:25
  88.1 18.5 %collective-permute-start.17 = (bf16[384,640]{1,0:T(8,128)(2,1)}, bf16[384,640]{1,0:T(8,128)(2,1)}, u32[]{:S(2)}, u32[]{:S(2)}) collective-permute-start(bf16[384,640]{1,0:T(8,128)(2,1)} %collective-permute-done.13.refs_7_), channel_id=1, source_target_pairs={{0,32},{32,0},{1,33},{33,1},{2,34},{34,2},{3,35},{35,3},{4,36},{36... | collective-permute-start | bytes 1474568 | tf_op jit(solution)/shard_map/ppermute | solution.py:25
  97.4 10.4 %collective-permute-start.22 = (f32[32,1024]{1,0:T(8,128)S(1)}, f32[32,1024]{1,0:T(8,128)S(1)}, u32[]{:S(2)}, u32[]{:S(2)}) collective-permute-start(f32[32,1024]{1,0:T(8,128)S(1)} %pad_maximum_fusion.2), channel_id=1, source_target_pairs={{0,16},{16,0},{1,17},{17,1},{2,18},{18,2},{3,19},{19,3},{4,20},{20... | collective-permute-start | bytes 393224 | tf_op jit(solution)/shard_map/ppermute | solution.py:25
  104.5 34.4 %copy-start.7 = (bf16[384,640]{1,0:T(8,128)(2,1)}, bf16[384,640]{1,0:T(8,128)(2,1)S(1)}, u32[]{:S(2)}) copy-start(bf16[384,640]{1,0:T(8,128)(2,1)S(1)} %collective-permute-done.15.refs_9_) | copy-start | bytes 1474564
  104.5 23.7 %collective-permute-start.8 = (bf16[4,160,1024]{2,1,0:T(8,128)(2,1)S(1)}, bf16[4,160,1024]{2,1,0:T(8,128)(2,1)}, u32[]{:S(2)}, u32[]{:S(2)}) collective-permute-start(bf16[4,160,1024]{2,1,0:T(8,128)(2,1)S(1)} %pad_maximum_fusion.1.refs_0_), channel_id=1, source_target_pairs={{0,4},{1,5},{2,6},{3,7},{4,8},{5,9},{6,10},{7,11},{8,12},{9,13},{1... | collective-permute-start | bytes 3932168 | tf_op jit(solution)/shard_map/ppermute | solution.py:51
  105.0 33.9 %collective-permute-start.9 = (bf16[4,160,1024]{2,1,0:T(8,128)(2,1)S(1)}, bf16[4,160,1024]{2,1,0:T(8,128)(2,1)}, u32[]{:S(2)}, u32[]{:S(2)}) collective-permute-start(bf16[4,160,1024]{2,1,0:T(8,128)(2,1)S(1)} %pad_maximum_fusion.1.refs_0_), channel_id=1, source_target_pairs={{0,8},{1,9},{2,10},{3,11},{4,12},{5,13},{6,14},{7,15},{8,0},{9,1},... | collective-permute-start | bytes 3932168 | tf_op jit(solution)/shard_map/ppermute | solution.py:51
  106.6 61.9 %collective-permute-start.18 = (bf16[4,160,1024]{2,1,0:T(8,128)(2,1)}, bf16[4,160,1024]{2,1,0:T(8,128)(2,1)}, u32[]{:S(2)}, u32[]{:S(2)}) collective-permute-start(bf16[4,160,1024]{2,1,0:T(8,128)(2,1)} %pad_maximum_fusion.a), channel_id=1, source_target_pairs={{0,4},{1,5},{2,6},{3,7},{4,8},{5,9},{6,10},{7,11},{8,12},{9,13},{1... | collective-permute-start | bytes 3932168 | tf_op jit(solution)/shard_map/ppermute | solution.py:51
  107.8 60.8 %collective-permute-start.19 = (bf16[4,160,1024]{2,1,0:T(8,128)(2,1)}, bf16[4,160,1024]{2,1,0:T(8,128)(2,1)}, u32[]{:S(2)}, u32[]{:S(2)}) collective-permute-start(bf16[4,160,1024]{2,1,0:T(8,128)(2,1)} %pad_maximum_fusion.a), channel_id=1, source_target_pairs={{0,12},{1,13},{2,14},{3,15},{4,0},{5,1},{6,2},{7,3},{8,4},{9,5},{1... | collective-permute-start | bytes 3932168 | tf_op jit(solution)/shard_map/ppermute | solution.py:51
  109.3 64.5 %collective-permute-start.4 = (bf16[4,160,1024]{2,1,0:T(8,128)(2,1)}, bf16[4,160,1024]{2,1,0:T(8,128)(2,1)}, u32[]{:S(2)}, u32[]{:S(2)}) collective-permute-start(bf16[4,160,1024]{2,1,0:T(8,128)(2,1)} %pad_maximum_fusion.a), channel_id=1, source_target_pairs={{0,8},{1,9},{2,10},{3,11},{4,12},{5,13},{6,14},{7,15},{8,0},{9,1},... | collective-permute-start | bytes 3932168 | tf_op jit(solution)/shard_map/ppermute | solution.py:51
  110.6 63.2 %all-to-all-start.3 = ((bf16[16,16,1024]{2,1,0:T(8,128)(2,1)}), bf16[16,16,1024]{2,1,0:T(8,128)(2,1)S(1)}, u32[]{:S(2)}, u32[]{:S(2)}) async-start(bf16[16,16,1024]{2,1,0:T(8,128)(2,1)} %broadcast_in_dim.5), calls=%async_computation.3 | async-start | bytes 1048576 | tf_op jit(solution)/shard_map/all_to_all | solution.py:29
  (8 other events, 56.0 us)
